TPU v7x, 32 devices: a whole 2x2x4 slice. The times are simulated.
32 devices in a mesh: section: 4 (over y, x), dp: 8 (over z, core).
Axes of the slice: x: 2, y: 2, z: 4, core: 2. Of those that a mesh axis runs over, the one named last changes fastest.
Arguments:
- big_crops: bfloat16 [8, 16, 14, 14, 384], P(None, 'dp'), may hold values from -6 to 6
- small_crops: bfloat16 [8, 48, 6, 6, 384], P(None, 'dp'), may hold values from -6 to 6
- big_cot: bfloat16 [8, 16, 7, 7, 768], P(None, 'dp'), may hold values from -6 to 6
- small_cot: bfloat16 [8, 48, 3, 3, 768], P(None, 'dp'), may hold values from -6 to 6
- drop_mask: int32 [8, 8], P(None, 'dp'), may hold values 0 or 1
- kernel_w: float32 [49, 384], P(None, 'dp'), may hold values from -4 to 4
- kernel_mom: float32 [49, 384], P(None, 'dp'), may hold values from -69.041437 to 69.041437
- kernel_avg: float32 [49, 384], P(None, 'dp'), may hold values from -4 to 4
- vector_w: float32 [13, 384], P(None, 'dp'), may hold values from -1 to 2
- vector_mom: float32 [13, 384], P(None, 'dp'), may hold values from -394.5225 to 394.5225
- vector_avg: float32 [13, 384], P(None, 'dp'), may hold values from -1 to 2
- up_w: float32 [384, 1536], P(None, 'dp'), may hold values from -4 to 4
- up_mom: float32 [384, 1536], P(None, 'dp'), may hold values from -10.066446 to 10.066446
- up_avg: float32 [384, 1536], P(None, 'dp'), may hold values from -4 to 4
- down_w: float32 [1536, 384], P('dp'), may hold values from -4 to 4
- down_mom: float32 [1536, 384], P('dp'), may hold values from -10.066446 to 10.066446
- down_avg: float32 [1536, 384], P('dp'), may hold values from -4 to 4
- strided_w: float32 [1536, 768], P('dp'), may hold values from -4 to 4
- strided_mom: float32 [1536, 768], P('dp'), may hold values from -10.066446 to 10.066446
- strided_avg: float32 [1536, 768], P('dp'), may hold values from -4 to 4
Outputs:
- out_big: float32 [8, 16, 7, 7, 768], P('section', 'dp')
- out_small: float32 [8, 48, 3, 3, 768], P('section', 'dp')
- grad_big: float32 [8, 16, 14, 14, 384], P('section', 'dp')
- grad_small: float32 [8, 48, 6, 6, 384], P('section', 'dp')
- kernel_next: float32 [49, 384], P(None, 'dp')
- kernel_mom_next: float32 [49, 384], P(None, 'dp')
- kernel_avg_next: float32 [49, 384], P(None, 'dp')
- vector_next: float32 [13, 384], P(None, 'dp')
- vector_mom_next: float32 [13, 384], P(None, 'dp')
- vector_avg_next: float32 [13, 384], P(None, 'dp')
- up_next: float32 [384, 1536], P(None, 'dp')
- up_mom_next: float32 [384, 1536], P(None, 'dp')
- up_avg_next: float32 [384, 1536], P(None, 'dp')
- down_next: float32 [1536, 384], P('dp')
- down_mom_next: float32 [1536, 384], P('dp')
- down_avg_next: float32 [1536, 384], P('dp')
- strided_next: float32 [1536, 768], P('dp')
- strided_mom_next: float32 [1536, 768], P('dp')
- strided_avg_next: float32 [1536, 768], P('dp')
All inputs are finite; a program needn't handle non-finite values. No bound on the sum of `drop_mask` on one device may be relied on, other than what follows from the above.
Results may differ from a plain program's by a relative error of at most 0.0094.
Values may be sent and summed in bfloat16 or wider, within the bound.
A program may use at most 192 MiB of HBM per device.

v0:
```python
import math

import jax
import jax.numpy as jnp
from jax import lax
from jax.sharding import PartitionSpec as P

C = 384
FF = 1536
C2 = 768
KS = 7
BIG_IMG = 2
SMALL_IMG = 6


KEEP_RATE = 0.9
MOMENTUM = 0.5
AVERAGING = 0.5
EPSILON = 1e-06
RATES = (1.1, 0.4, 2.7, 1.3, 1.3)
HIGHEST = lax.Precision.HIGHEST


def shifted(shard, axis, by):
    peers = lax.axis_size(axis)
    pairs = [(i, i + by) for i in range(peers) if 0 <= i + by < peers]
    return lax.ppermute(shard, axis, pairs)


def layer_norm(values, gain_row, offset_row):
    average = jnp.mean(values, axis=-1, keepdims=True)
    centered = values - average
    variance = jnp.mean(centered * centered, axis=-1, keepdims=True)
    return centered * lax.rsqrt(variance + EPSILON) * gain_row + offset_row


def depthwise(crop_field, kernel, exact_mode):
    radius = KS // 2
    channels = crop_field.shape[-1]
    if exact_mode:
        return lax.conv_general_dilated(
            crop_field,
            kernel.reshape(KS, KS, 1, channels),
            (1, 1),
            ((radius, radius), (radius, radius)),
            dimension_numbers=("NHWC", "HWIO", "NHWC"),
            feature_group_count=channels,
            precision=HIGHEST,
        )
    return lax.conv_general_dilated(
        crop_field,
        kernel.reshape(KS, KS, 1, channels),
        (1, 1),
        ((radius, radius), (radius, radius)),
        dimension_numbers=("NHWC", "HWIO", "NHWC"),
        feature_group_count=channels,
        preferred_element_type=jnp.float32,
    )


def gelu_exact(values):
    return jax.nn.gelu(values, approximate=False)


def to_blocks(crop_field):
    crop_count, crop_side = (crop_field.shape[0], crop_field.shape[1])
    half_side = crop_side // 2
    return (
        crop_field.reshape(crop_count, half_side, 2, half_side, 2, C)
        .transpose(0, 1, 3, 2, 4, 5)
        .reshape(crop_count * half_side * half_side, 4 * C)
    )


def from_blocks(flat_blocks, crop_shape):
    crop_count, crop_side = (crop_shape[0], crop_shape[1])
    half_side = crop_side // 2
    return (
        flat_blocks.reshape(crop_count, half_side, half_side, 2, 2, C)
        .transpose(0, 1, 3, 2, 4, 5)
        .reshape(crop_shape)
    )


def contract(left_side, right_side):
    return lax.dot_general(
        left_side, right_side, (((0,), (0,)), ((), ())), preferred_element_type=jnp.float32
    )


def take_slot(buffer, slot_index):
    return lax.dynamic_index_in_dim(buffer, slot_index, 0, keepdims=False)


def put_slot(buffer, entry_value, slot_index, is_active):
    old_entry = take_slot(buffer, slot_index)
    return lax.dynamic_update_index_in_dim(
        buffer, jnp.where(is_active, entry_value, old_entry), slot_index, 0
    )


def keep_rows(keep_crop, crop_side):
    return jnp.repeat(keep_crop, crop_side * crop_side)[:, None]


def body(
    big_crops,
    small_crops,
    big_cot,
    small_cot,
    drop_mask,
    kernel_w,
    kernel_mom,
    kernel_avg,
    vector_w,
    vector_mom,
    vector_avg,
    up_w,
    up_mom,
    up_avg,
    down_w,
    down_mom,
    down_avg,
    strided_w,
    strided_mom,
    strided_avg,
):
    kernel, vector, up_full, down_full, strided = (
        lax.all_gather(kernel_w.astype(jnp.bfloat16), "dp", axis=1, tiled=True),
        lax.all_gather(vector_w.astype(jnp.bfloat16), "dp", axis=1, tiled=True),
        lax.all_gather(up_w.astype(jnp.bfloat16), "dp", axis=1, tiled=True),
        lax.all_gather(down_w.astype(jnp.bfloat16), "dp", axis=0, tiled=True),
        lax.all_gather(strided_w.astype(jnp.bfloat16), "dp", axis=0, tiled=True),
    )
    values = vector.astype(jnp.float32)
    up_rows = FF // C
    half_rows = up_rows // 2
    half_ff = FF // 2
    bias_dw = values[0]
    gain_one = values[1]
    offset_one = values[2]
    bias_first = values[3 : 3 + half_rows].reshape(half_ff)
    bias_second = values[3 + half_rows : 3 + up_rows].reshape(half_ff)
    bias_down = values[3 + up_rows]
    layer_scale = values[4 + up_rows]
    gain_two = values[5 + up_rows]
    offset_two = values[6 + up_rows]
    bias_out = values[7 + up_rows :].reshape(C2)
    up_first = up_full[:, :half_ff]
    up_second = up_full[:, half_ff:]
    down_first = down_full[:half_ff]
    down_second = down_full[half_ff:]
    kernel_scale = 1.0 / KS
    up_scale = 1.0 / math.sqrt(C)
    down_scale = 1.0 / math.sqrt(FF)
    strided_scale = 1.0 / math.sqrt(4 * C)
    keep_image = drop_mask.astype(jnp.float32) / KEEP_RATE
    keep_big = jnp.repeat(keep_image, BIG_IMG, axis=1)
    keep_small = jnp.repeat(keep_image, SMALL_IMG, axis=1)
    big_shape = big_crops.shape[1:]
    small_shape = small_crops.shape[1:]
    zero_narrow = (jnp.zeros(big_shape, jnp.bfloat16), jnp.zeros(small_shape, jnp.bfloat16))
    zero_wide = (jnp.zeros(big_shape, jnp.float32), jnp.zeros(small_shape, jnp.float32))
    zero_result = (
        jnp.zeros(big_cot.shape[1:], jnp.float32),
        jnp.zeros(small_cot.shape[1:], jnp.float32),
    )
    zero_totals = (
        jnp.zeros(kernel.shape, jnp.float32),
        jnp.zeros(vector.shape, jnp.float32),
        jnp.zeros(up_full.shape, jnp.float32),
        jnp.zeros(down_full.shape, jnp.float32),
        jnp.zeros(strided.shape, jnp.float32),
    )

    def first_part(crop_field):
        conv_out = depthwise(crop_field, kernel, False) * kernel_scale + bias_dw
        return layer_norm(conv_out, gain_one, offset_one).astype(jnp.bfloat16)

    def second_part(normed):
        flat_rows = normed.reshape(-1, C)
        pre_act = (
            jnp.dot(flat_rows, up_first, preferred_element_type=jnp.float32) * up_scale + bias_first
        )
        hidden = gelu_exact(pre_act).astype(jnp.bfloat16)
        return jnp.dot(hidden, down_first, preferred_element_type=jnp.float32).reshape(normed.shape)

    def branch_value(normed, partial_sum):
        flat_rows = normed.reshape(-1, C)
        pre_act = (
            jnp.dot(flat_rows, up_second, preferred_element_type=jnp.float32) * up_scale
            + bias_second
        )
        activated, gelu_pull = jax.vjp(gelu_exact, pre_act)
        hidden = activated.astype(jnp.bfloat16)
        branch = (
            partial_sum.reshape(-1, C)
            + jnp.dot(hidden, down_second, preferred_element_type=jnp.float32)
        ) * down_scale + bias_down
        return (flat_rows, hidden, gelu_pull, branch)

    def third_part(normed, partial_sum, crop_field, keep_crop):
        flat_rows, hidden, gelu_pull, branch = branch_value(normed, partial_sum)
        factor = keep_rows(keep_crop, crop_field.shape[1])
        mixed_sum = crop_field.reshape(-1, C).astype(jnp.float32) + layer_scale * branch * factor
        return (
            layer_norm(mixed_sum, gain_two, offset_two)
            .astype(jnp.bfloat16)
            .reshape(crop_field.shape)
        )

    def fourth_part(zeta_norm):
        crop_count, crop_side = (zeta_norm.shape[0], zeta_norm.shape[1])
        result = (
            jnp.dot(to_blocks(zeta_norm), strided, preferred_element_type=jnp.float32)
            * strided_scale
            + bias_out
        )
        return result.reshape(crop_count, crop_side // 2, crop_side // 2, C2)

    def first_back(crop_field, d_normed):

        def local_piece(field_value, kernel_value, bias_value, gain_value, offset_value):
            conv_out = depthwise(field_value, kernel_value, True) * kernel_scale + bias_value
            return layer_norm(conv_out, gain_value, offset_value)

        primal, pullback = jax.vjp(
            local_piece,
            crop_field.astype(jnp.float32),
            kernel.astype(jnp.float32),
            bias_dw,
            gain_one,
            offset_one,
        )
        return pullback(d_normed.astype(jnp.float32))

    def second_back(normed, d_branch, d_part):
        flat_rows = normed.reshape(-1, C)
        pre_act = (
            jnp.dot(flat_rows, up_first, preferred_element_type=jnp.float32) * up_scale + bias_first
        )
        activated, gelu_pull = jax.vjp(gelu_exact, pre_act)
        hidden = activated.astype(jnp.bfloat16)
        grad_rows = d_branch.reshape(-1, C)
        d_down = contract(hidden, grad_rows) * down_scale
        d_hidden = (
            jnp.einsum("rc,hc->rh", grad_rows, down_first, preferred_element_type=jnp.float32)
            * down_scale
        )
        d_pre = gelu_pull(d_hidden)[0].astype(jnp.bfloat16)
        d_bias = jnp.sum(d_pre.astype(jnp.float32), axis=0)
        d_up = contract(flat_rows, d_pre) * up_scale
        d_normed = (
            d_part.reshape(-1, C)
            + jnp.einsum("rh,ch->rc", d_pre, up_first, preferred_element_type=jnp.float32)
            * up_scale
        )
        return (d_normed.astype(jnp.bfloat16).reshape(normed.shape), d_up, d_bias, d_down)

    def third_back(normed, partial_sum, crop_field, keep_crop, d_zeta):
        flat_rows, hidden, gelu_pull, branch = branch_value(normed, partial_sum)
        factor = keep_rows(keep_crop, crop_field.shape[1])
        mixed_sum = crop_field.reshape(-1, C).astype(jnp.float32) + layer_scale * branch * factor
        primal, norm_pull = jax.vjp(layer_norm, mixed_sum, gain_two, offset_two)
        d_mixed, d_gain, d_offset = norm_pull(d_zeta.reshape(-1, C).astype(jnp.float32))
        d_scale = jnp.sum(d_mixed * factor * branch, axis=0)
        d_branch = (d_mixed * factor * layer_scale).astype(jnp.bfloat16)
        d_bias_down = jnp.sum(d_branch.astype(jnp.float32), axis=0)
        d_down = contract(hidden, d_branch) * down_scale
        d_hidden = (
            jnp.einsum("rc,hc->rh", d_branch, down_second, preferred_element_type=jnp.float32)
            * down_scale
        )
        d_pre = gelu_pull(d_hidden)[0].astype(jnp.bfloat16)
        d_bias = jnp.sum(d_pre.astype(jnp.float32), axis=0)
        d_up = contract(flat_rows, d_pre) * up_scale
        d_part = (
            jnp.einsum("rh,ch->rc", d_pre, up_second, preferred_element_type=jnp.float32) * up_scale
        )
        return (
            d_branch.reshape(crop_field.shape),
            d_part.reshape(crop_field.shape),
            d_mixed.reshape(crop_field.shape),
            d_gain,
            d_offset,
            d_scale,
            d_bias_down,
            d_down,
            d_bias,
            d_up,
        )

    def fourth_back(zeta_norm, cotangent):
        grad_out = cotangent.reshape(-1, C2)
        blocks = to_blocks(zeta_norm)
        d_strided = contract(blocks, grad_out) * strided_scale
        d_bias_out = jnp.sum(grad_out.astype(jnp.float32), axis=0)
        d_blocks = (
            jnp.einsum("ro,ko->rk", grad_out, strided, preferred_element_type=jnp.float32)
            * strided_scale
        )
        return (from_blocks(d_blocks, zeta_norm.shape).astype(jnp.bfloat16), d_strided, d_bias_out)

    def section_zero(slot_index, narrow, wide):
        return (
            (
                first_part(take_slot(big_crops, slot_index)),
                first_part(take_slot(small_crops, slot_index)),
            ),
            zero_wide,
            zero_result,
        )

    def section_one(slot_index, narrow, wide):
        return (narrow, (second_part(narrow[0]), second_part(narrow[1])), zero_result)

    def section_two(slot_index, narrow, wide):
        zeta_big = third_part(
            narrow[0], wide[0], take_slot(big_crops, slot_index), take_slot(keep_big, slot_index)
        )
        zeta_small = third_part(
            narrow[1],
            wide[1],
            take_slot(small_crops, slot_index),
            take_slot(keep_small, slot_index),
        )
        return ((zeta_big, zeta_small), zero_wide, zero_result)

    def section_three(slot_index, narrow, wide):
        return (zero_narrow, zero_wide, (fourth_part(narrow[0]), fourth_part(narrow[1])))

    def section_spare(slot_index, narrow, wide):
        return (zero_narrow, zero_wide, zero_result)

    def back_zero(slot_index, saved_narrow, saved_wide, grad_narrow, grad_wide, totals):
        big_parts = first_back(take_slot(big_crops, slot_index), grad_narrow[0])
        small_parts = first_back(take_slot(small_crops, slot_index), grad_narrow[1])
        vector_grad = (
            totals[1]
            .at[0]
            .add(big_parts[2] + small_parts[2])
            .at[1]
            .add(big_parts[3] + small_parts[3])
            .at[2]
            .add(big_parts[4] + small_parts[4])
        )
        totals = (
            totals[0] + big_parts[1] + small_parts[1],
            vector_grad,
            totals[2],
            totals[3],
            totals[4],
        )
        return (zero_narrow, zero_wide, totals, (big_parts[0], small_parts[0]))

    def back_one(slot_index, saved_narrow, saved_wide, grad_narrow, grad_wide, totals):
        big_parts = second_back(saved_narrow[0], grad_narrow[0], grad_wide[0])
        small_parts = second_back(saved_narrow[1], grad_narrow[1], grad_wide[1])
        vector_grad = (
            totals[1]
            .at[3 : 3 + half_rows]
            .add((big_parts[2] + small_parts[2]).reshape(half_rows, C))
        )
        totals = (
            totals[0],
            vector_grad,
            totals[2].at[:, :half_ff].add(big_parts[1] + small_parts[1]),
            totals[3].at[:half_ff].add(big_parts[3] + small_parts[3]),
            totals[4],
        )
        return ((big_parts[0], small_parts[0]), zero_wide, totals, zero_wide)

    def back_two(slot_index, saved_narrow, saved_wide, grad_narrow, grad_wide, totals):
        big_parts = third_back(
            saved_narrow[0],
            saved_wide[0],
            take_slot(big_crops, slot_index),
            take_slot(keep_big, slot_index),
            grad_narrow[0],
        )
        small_parts = third_back(
            saved_narrow[1],
            saved_wide[1],
            take_slot(small_crops, slot_index),
            take_slot(keep_small, slot_index),
            grad_narrow[1],
        )
        d_gain, d_offset, d_scale, d_bias_down, d_down, d_bias, d_up = tuple(
            (running + addend for running, addend in zip(big_parts[3:], small_parts[3:]))
        )
        vector_grad = (
            totals[1]
            .at[3 + half_rows : 3 + up_rows]
            .add(d_bias.reshape(half_rows, C))
            .at[3 + up_rows]
            .add(d_bias_down)
            .at[4 + up_rows]
            .add(d_scale)
            .at[5 + up_rows]
            .add(d_gain)
            .at[6 + up_rows]
            .add(d_offset)
        )
        totals = (
            totals[0],
            vector_grad,
            totals[2].at[:, half_ff:].add(d_up),
            totals[3].at[half_ff:].add(d_down),
            totals[4],
        )
        return (
            (big_parts[0], small_parts[0]),
            (big_parts[1], small_parts[1]),
            totals,
            (big_parts[2], small_parts[2]),
        )

    def back_three(slot_index, saved_narrow, saved_wide, grad_narrow, grad_wide, totals):
        big_parts = fourth_back(saved_narrow[0], take_slot(big_cot, slot_index))
        small_parts = fourth_back(saved_narrow[1], take_slot(small_cot, slot_index))
        vector_grad = (
            totals[1].at[7 + up_rows :].add((big_parts[2] + small_parts[2]).reshape(C2 // C, C))
        )
        totals = (
            totals[0],
            vector_grad,
            totals[2],
            totals[3],
            totals[4] + big_parts[1] + small_parts[1],
        )
        return ((big_parts[0], small_parts[0]), zero_wide, totals, zero_wide)

    def back_spare(slot_index, saved_narrow, saved_wide, grad_narrow, grad_wide, totals):
        return (zero_narrow, zero_wide, totals, zero_wide)

    forward_list = [section_zero, section_one, section_two, section_three]
    backward_list = [back_zero, back_one, back_two, back_three]
    micro_count = big_crops.shape[0]
    sections = lax.axis_size("section")
    section_rank = lax.axis_index("section")
    shard_grads = None
    store_narrow_init = (
        jnp.zeros(big_crops.shape, jnp.bfloat16),
        jnp.zeros(small_crops.shape, jnp.bfloat16),
    )
    store_wide_init = (
        jnp.zeros(big_crops.shape, jnp.float32),
        jnp.zeros(small_crops.shape, jnp.float32),
    )
    results_init = (jnp.zeros(big_cot.shape, jnp.float32), jnp.zeros(small_cot.shape, jnp.float32))
    terms_init = (
        jnp.zeros(big_crops.shape, jnp.float32),
        jnp.zeros(small_crops.shape, jnp.float32),
    )
    ticks = jnp.arange(micro_count + sections - 1, dtype=jnp.int32)

    def ahead(loop_state, clock_tick):
        recv_narrow, recv_wide, store_narrow, store_wide, results = loop_state
        micro_index = clock_tick - section_rank
        is_active = (micro_index >= 0) & (micro_index < micro_count)
        slot_index = jnp.clip(micro_index, 0, micro_count - 1)
        store_narrow = (
            put_slot(store_narrow[0], recv_narrow[0], slot_index, is_active),
            put_slot(store_narrow[1], recv_narrow[1], slot_index, is_active),
        )
        store_wide = (
            put_slot(store_wide[0], recv_wide[0], slot_index, is_active),
            put_slot(store_wide[1], recv_wide[1], slot_index, is_active),
        )
        sent_narrow, sent_wide, produced = lax.switch(
            jnp.where(is_active, section_rank, sections),
            forward_list + [section_spare],
            slot_index,
            recv_narrow,
            recv_wide,
        )
        results = (
            put_slot(results[0], produced[0], slot_index, is_active),
            put_slot(results[1], produced[1], slot_index, is_active),
        )
        moved = shifted(
            (
                sent_narrow[0].astype(jnp.float32),
                sent_narrow[1].astype(jnp.float32),
                sent_wide[0],
                sent_wide[1],
            ),
            "section",
            1,
        )
        recv_narrow = (moved[0].astype(jnp.bfloat16), moved[1].astype(jnp.bfloat16))
        recv_wide = (moved[2], moved[3])
        return ((recv_narrow, recv_wide, store_narrow, store_wide, results), None)

    loop_state, unused = lax.scan(
        ahead, (zero_narrow, zero_wide, store_narrow_init, store_wide_init, results_init), ticks
    )
    store_narrow, store_wide, results = (loop_state[2], loop_state[3], loop_state[4])

    def behind(loop_state, clock_tick):
        recv_narrow, recv_wide, totals, grad_terms = loop_state
        micro_index = clock_tick - (sections - 1 - section_rank)
        is_active = (micro_index >= 0) & (micro_index < micro_count)
        slot_index = jnp.clip(micro_index, 0, micro_count - 1)
        saved_narrow = (
            take_slot(store_narrow[0], slot_index),
            take_slot(store_narrow[1], slot_index),
        )
        saved_wide = (take_slot(store_wide[0], slot_index), take_slot(store_wide[1], slot_index))
        sent_narrow, sent_wide, totals, produced = lax.switch(
            jnp.where(is_active, section_rank, sections),
            backward_list + [back_spare],
            slot_index,
            saved_narrow,
            saved_wide,
            recv_narrow,
            recv_wide,
            totals,
        )
        grad_terms = (
            put_slot(grad_terms[0], produced[0], slot_index, is_active),
            put_slot(grad_terms[1], produced[1], slot_index, is_active),
        )
        moved = shifted(
            (
                sent_narrow[0].astype(jnp.float32),
                sent_narrow[1].astype(jnp.float32),
                sent_wide[0],
                sent_wide[1],
            ),
            "section",
            -1,
        )
        recv_narrow = (moved[0].astype(jnp.bfloat16), moved[1].astype(jnp.bfloat16))
        recv_wide = (moved[2], moved[3])
        return ((recv_narrow, recv_wide, totals, grad_terms), None)

    loop_state, unused = lax.scan(behind, (zero_narrow, zero_wide, zero_totals, terms_init), ticks)
    totals, grad_terms = (loop_state[2], loop_state[3])
    out_big, out_small, grad_big, grad_small = (
        lax.psum_scatter(results[0], "section", scatter_dimension=0, tiled=True),
        lax.psum_scatter(results[1], "section", scatter_dimension=0, tiled=True),
        lax.psum_scatter(grad_terms[0], "section", scatter_dimension=0, tiled=True),
        lax.psum_scatter(grad_terms[1], "section", scatter_dimension=0, tiled=True),
    )
    dp_rank = lax.axis_index("dp")
    whole = lax.psum((totals[0], totals[1], totals[2], totals[3], totals[4]), ("section", "dp"))
    shard_grads = (
        lax.dynamic_slice_in_dim(whole[0], dp_rank * kernel_w.shape[1], kernel_w.shape[1], 1),
        lax.dynamic_slice_in_dim(whole[1], dp_rank * vector_w.shape[1], vector_w.shape[1], 1),
        lax.dynamic_slice_in_dim(whole[2], dp_rank * up_w.shape[1], up_w.shape[1], 1),
        lax.dynamic_slice_in_dim(whole[3], dp_rank * down_w.shape[0], down_w.shape[0], 0),
        lax.dynamic_slice_in_dim(whole[4], dp_rank * strided_w.shape[0], strided_w.shape[0], 0),
    )
    pixel_total = (
        lax.axis_size("dp")
        * micro_count
        * (
            big_crops.shape[1] * big_crops.shape[2] * big_crops.shape[3]
            + small_crops.shape[1] * small_crops.shape[2] * small_crops.shape[3]
        )
    )
    fans = (KS * KS, 1, C, FF, 4 * C)
    masters = (kernel_w, vector_w, up_w, down_w, strided_w)
    moments = (kernel_mom, vector_mom, up_mom, down_mom, strided_mom)
    averages = (kernel_avg, vector_avg, up_avg, down_avg, strided_avg)
    updates = []
    for position in range(5):
        step_rate = RATES[position] * math.sqrt(fans[position] / pixel_total)
        moment_next = MOMENTUM * moments[position] + shard_grads[position]
        weight_next = masters[position] - step_rate * (
            shard_grads[position] + MOMENTUM * moment_next
        )
        average_next = AVERAGING * averages[position] + (1.0 - AVERAGING) * weight_next
        updates.append((weight_next, moment_next, average_next))
    return (
        out_big,
        out_small,
        grad_big,
        grad_small,
        updates[0][0],
        updates[0][1],
        updates[0][2],
        updates[1][0],
        updates[1][1],
        updates[1][2],
        updates[2][0],
        updates[2][1],
        updates[2][2],
        updates[3][0],
        updates[3][1],
        updates[3][2],
        updates[4][0],
        updates[4][1],
        updates[4][2],
    )


def solution(mesh):
    in_specs = (
        P(None, "dp", None, None, None),
        P(None, "dp", None, None, None),
        P(None, "dp", None, None, None),
        P(None, "dp", None, None, None),
        P(None, "dp"),
        P(None, "dp"),
        P(None, "dp"),
        P(None, "dp"),
        P(None, "dp"),
        P(None, "dp"),
        P(None, "dp"),
        P(None, "dp"),
        P(None, "dp"),
        P(None, "dp"),
        P("dp", None),
        P("dp", None),
        P("dp", None),
        P("dp", None),
        P("dp", None),
        P("dp", None),
    )
    out_specs = (
        P("section", "dp", None, None, None),
        P("section", "dp", None, None, None),
        P("section", "dp", None, None, None),
        P("section", "dp", None, None, None),
        P(None, "dp"),
        P(None, "dp"),
        P(None, "dp"),
        P(None, "dp"),
        P(None, "dp"),
        P(None, "dp"),
        P(None, "dp"),
        P(None, "dp"),
        P(None, "dp"),
        P("dp", None),
        P("dp", None),
        P("dp", None),
        P("dp", None),
        P("dp", None),
        P("dp", None),
    )
    return jax.shard_map(body, mesh=mesh, in_specs=in_specs, out_specs=out_specs, check_vma=False)
```

profile of v0, /device:TPU:0, one launch (start us, length us, event | category | flops | bytes accessed | tf_op | source)
XLA Modules:
  0.0 2764.2 jit_solution(2891305932265503693)
XLA Ops:
  15.4 15.8 all_gather.15
  63.1 31.3 %all-gather.9.cloned.1.call-done = bf16[1536,768]{1,0:T(8,128)(2,1)} async-done(((bf16[192,768]{1,0:T(8,128)(2,1)}), bf16[1536,768]{1,0:T(8,128)(2,1)}) %all-gather.9.cloned.1.call-update) | async-done | bytes 2359312 | tf_op jit(solution)/shard_map/all_gather | solution.py:133
  109.2 906.7 %while.79 = (s32[]{:T(128)}, bf16[2,14,14,384]{3,0,2,1:T(2,128)(2,1)}, bf16[6,6,6,384]{3,2,1,0:T(8,128)(2,1)}, f32[2,14,14,384]{3,0,2,1:T(2,128)}, f32[6,6,6,384...) while((s32[]{:T(128)}, ...), condition=%wide.region_14.15_spmd.clone.clone.clone, body=%wide.region_0.14_spmd.clone.clone.clone.sunk | while | flops 753064512 | bytes 43560756 | solution.py:495
  132.9 24.4 conditional.10
  177.3 15.7 collective-permute-done.3
  204.0 24.4 conditional.10
  248.5 15.2 collective-permute-done.3
  274.7 24.4 conditional.10
  301.1 19.0 collective-permute-start.1
  357.5 24.4 conditional.10
  383.8 26.2 collective-permute-start.1
  447.2 24.4 conditional.10
  473.6 25.5 collective-permute-start.1
  536.3 24.4 conditional.10
  562.7 24.6 collective-permute-start.1
  624.0 24.4 conditional.10
  650.4 24.3 collective-permute-start.1
  710.3 24.4 conditional.10
  736.7 24.2 collective-permute-start.1
  801.1 19.7 collective-permute-start
  820.9 26.3 collective-permute-start.1
  893.0 40.4 %collective-permute-start.1 = (bf16[6,6,6,384]{3,2,1,0:T(8,128)(2,1)}, bf16[6,6,6,384]{3,2,1,0:T(8,128)(2,1)S(1)}, u32[]{:S(2)}, u32[]{:S(2)}) collective-permute-start(bf16[6,6,6,384]{3,2,1,0:T(8,128)(2,1)} %get-tuple-element.3839), channel_id=1, source_target_pairs={{0,8},{8,16},{16,24},{1,9},{9,17},{17,25},{2,10},{10,18},{18,26},{... | collective-permute-start | bytes 497672 | tf_op jit(solution)/shard_map/while/body/eval_jaxpr/ppermute | solution.py:27
  1035.3 1372.0 %while.80 = (s32[]{:T(128)}, bf16[2,14,14,384]{3,0,2,1:T(2,128)(2,1)}, bf16[6,6,6,384]{3,2,1,0:T(8,128)(2,1)}, f32[2,14,14,384]{3,0,2,1:T(2,128)}, f32[6,6,6,384...) while((s32[]{:T(128)}, ...), condition=%wide.region_60.61_spmd.clone.clone.clone, body=%wide.region_17.60_spmd.clone.clone.clone.sunk | while | flops 2201780480 | bytes 129214416 | solution.py:538
  1049.5 22.3 conditional.11
  1097.3 22.8 collective-permute-done.7
  1127.6 16.9 conditional.11
  1167.1 16.8 collective-permute-done.7
  1191.5 21.7 conditional.11
  1226.6 143.9 %collective-permute-done.5 = bf16[6,6,6,384]{3,2,1,0:T(8,128)(2,1)S(1)} collective-permute-done((bf16[6,6,6,384]{3,2,1,0:T(8,128)(2,1)}, bf16[6,6,6,384]{3,2,1,0:T(8,128)(2,1)S(1)}, u32[]{:S(2)}, u32[]{:S(2)}) %collective-permute-start.5) | collective-permute-done | bytes 165920 | tf_op jit(solution)/shard_map/while/body/eval_jaxpr/ppermute | solution.py:27
  1391.9 71.7 %conditional.11 = (bf16[6,6,6,384]{3,2,1,0:T(8,128)(2,1)}, f32[2,14,14,384]{3,2,1,0:T(8,128)}, f32[6,6,6,384]{3,2,1,0:T(8,128)}, f32[49,384]{1,0:T(8,128)}, f32[...) conditional(s32[]{:T(128)} %clamp.16, (s32[]{:T(128)}, ...), branch_computations={%region_18.32_spmd, %region_33.36_spmd, %region_37.55_spmd, %regio... | conditional | flops 2201313536 | bytes 108266576 | solution.py:510
  1478.3 24.0 collective-permute-done.5
  1523.3 71.7 %conditional.11 = (bf16[6,6,6,384]{3,2,1,0:T(8,128)(2,1)}, f32[2,14,14,384]{3,2,1,0:T(8,128)}, f32[6,6,6,384]{3,2,1,0:T(8,128)}, f32[49,384]{1,0:T(8,128)}, f32[...) conditional(s32[]{:T(128)} %clamp.16, (s32[]{:T(128)}, ...), branch_computations={%region_18.32_spmd, %region_33.36_spmd, %region_37.55_spmd, %regio... | conditional | flops 2201313536 | bytes 108266576 | solution.py:510
  1609.7 23.0 collective-permute-done.5
  1653.5 71.8 %conditional.11 = (bf16[6,6,6,384]{3,2,1,0:T(8,128)(2,1)}, f32[2,14,14,384]{3,2,1,0:T(8,128)}, f32[6,6,6,384]{3,2,1,0:T(8,128)}, f32[49,384]{1,0:T(8,128)}, f32[...) conditional(s32[]{:T(128)} %clamp.16, (s32[]{:T(128)}, ...), branch_computations={%region_18.32_spmd, %region_33.36_spmd, %region_37.55_spmd, %regio... | conditional | flops 2201313536 | bytes 108266576 | solution.py:510
  1740.0 23.6 collective-permute-done.5
  1784.1 71.7 %conditional.11 = (bf16[6,6,6,384]{3,2,1,0:T(8,128)(2,1)}, f32[2,14,14,384]{3,2,1,0:T(8,128)}, f32[6,6,6,384]{3,2,1,0:T(8,128)}, f32[49,384]{1,0:T(8,128)}, f32[...) conditional(s32[]{:T(128)} %clamp.16, (s32[]{:T(128)}, ...), branch_computations={%region_18.32_spmd, %region_33.36_spmd, %region_37.55_spmd, %regio... | conditional | flops 2201313536 | bytes 108266576 | solution.py:510
  1870.4 24.0 collective-permute-done.5
  1914.7 71.7 %conditional.11 = (bf16[6,6,6,384]{3,2,1,0:T(8,128)(2,1)}, f32[2,14,14,384]{3,2,1,0:T(8,128)}, f32[6,6,6,384]{3,2,1,0:T(8,128)}, f32[49,384]{1,0:T(8,128)}, f32[...) conditional(s32[]{:T(128)} %clamp.16, (s32[]{:T(128)}, ...), branch_computations={%region_18.32_spmd, %region_33.36_spmd, %region_37.55_spmd, %regio... | conditional | flops 2201313536 | bytes 108266576 | solution.py:510
  2001.2 22.9 collective-permute-done.5
  2044.1 71.7 %conditional.11 = (bf16[6,6,6,384]{3,2,1,0:T(8,128)(2,1)}, f32[2,14,14,384]{3,2,1,0:T(8,128)}, f32[6,6,6,384]{3,2,1,0:T(8,128)}, f32[49,384]{1,0:T(8,128)}, f32[...) conditional(s32[]{:T(128)} %clamp.16, (s32[]{:T(128)}, ...), branch_computations={%region_18.32_spmd, %region_33.36_spmd, %region_37.55_spmd, %regio... | conditional | flops 2201313536 | bytes 108266576 | solution.py:510
  2130.5 23.6 collective-permute-done.5
  2173.8 71.7 %conditional.11 = (bf16[6,6,6,384]{3,2,1,0:T(8,128)(2,1)}, f32[2,14,14,384]{3,2,1,0:T(8,128)}, f32[6,6,6,384]{3,2,1,0:T(8,128)}, f32[49,384]{1,0:T(8,128)}, f32[...) conditional(s32[]{:T(128)} %clamp.16, (s32[]{:T(128)}, ...), branch_computations={%region_18.32_spmd, %region_33.36_spmd, %region_37.55_spmd, %regio... | conditional | flops 2201313536 | bytes 108266576 | solution.py:510
  2260.1 24.0 collective-permute-done.5
  2303.5 71.8 %conditional.11 = (bf16[6,6,6,384]{3,2,1,0:T(8,128)(2,1)}, f32[2,14,14,384]{3,2,1,0:T(8,128)}, f32[6,6,6,384]{3,2,1,0:T(8,128)}, f32[49,384]{1,0:T(8,128)}, f32[...) conditional(s32[]{:T(128)} %clamp.16, (s32[]{:T(128)}, ...), branch_computations={%region_18.32_spmd, %region_33.36_spmd, %region_37.55_spmd, %regio... | conditional | flops 2201313536 | bytes 108266576 | solution.py:510
  2411.9 72.8 %psum.36 = f32[13,384]{1,0:T(8,128)S(1)} all-reduce(f32[13,384]{1,0:T(8,128)S(1)} %get-tuple-element.1123), channel_id=1, replica_groups=mesh['section'=4,'dp'=8] {'section','dp'}, use_global_device_ids=true, to_apply=%region_64.65 | all-reduce | flops 4992 | bytes 39936 | tf_op jit(solution)/shard_map/psum | solution.py:547
  2489.3 147.0 %all-reduce.7.cloned.1.call-done = (f32[49,384]{0,1:T(8,128)}, f32[384,1536]{0,1:T(8,128)}, f32[1536,384]{1,0:T(8,128)}, f32[1536,768]{1,0:T(8,128)}) async-done(((f32[49,384]{0,1:T(8,128)}, f32[384,1536]{0,1:T(8,128)}, f32[1536,384]{1,0:T(8,128)}, f32[1536,768]{1,0:T(8,128)}), (f32[49,384]{0,1:T(8,128)}, f32[384,1536]{0,1:T(8,128)}, f32[1536,384]{1,0:T(8,128)}, ...) | async-done | bytes 9512464 | tf_op jit(solution)/shard_map/psum | solution.py:547
  2644.2 42.7 %reduce-scatter.8.cloned.1.call-done = f32[2,6,6,6,384]{4,3,2,1,0:T(8,128)} async-done(((f32[8,6,6,6,384]{4,3,2,1,0:T(8,128)}), f32[2,6,6,6,384]{4,3,2,1,0:T(8,128)}) %reduce-scatter.8.cloned.1.call-update) | async-done | bytes 663568 | tf_op jit(solution)/shard_map/reduce_scatter | solution.py:544
  2689.4 64.4 %reduce-scatter.6.cloned.1.call-done = f32[2,2,14,14,384]{4,3,2,1,0:T(8,128)} async-done(((f32[8,2,14,14,384]{4,3,2,1,0:T(8,128)}), f32[2,2,14,14,384]{4,3,2,1,0:T(8,128)}) %reduce-scatter.6.cloned.1.call-update) | async-done | bytes 1204240 | tf_op jit(solution)/shard_map/reduce_scatter | solution.py:543
  (1713 shorter events, 1560.7 us)
Async XLA Ops:
  7.2 40.9 %all-gather.5.cloned.1.call-start = ((), (), s32[]{:S(2)}) async-start(), calls=%async_computation.3 | async-start | bytes 1327104 | tf_op jit(solution)/shard_map/all_gather | solution.py:131
  9.0 51.8 %all-gather.7.cloned.1.call-start = ((), (), s32[]{:S(2)}) async-start(), calls=%async_computation.4 | async-start | bytes 1327104 | tf_op jit(solution)/shard_map/all_gather | solution.py:132
  10.7 83.7 %all-gather.9.cloned.1.call-start = ((), (), s32[]{:S(2)}) async-start(), calls=%async_computation.5 | async-start | bytes 2654208 | tf_op jit(solution)/shard_map/all_gather | solution.py:133
  11.5 2473.9 %all-reduce.5.cloned.1.call-start = ((), (), s32[]{:S(2)}) async-start(), calls=%async_computation.9 | async-start | bytes 4816896
  157.2 39.7 %collective-permute-start = (bf16[2,14,14,384]{3,0,2,1:T(2,128)(2,1)}, bf16[2,14,14,384]{3,0,2,1:T(2,128)(2,1)}, u32[]{:S(2)}, u32[]{:S(2)}) collective-permute-start(bf16[2,14,14,384]{3,0,2,1:T(2,128)(2,1)} %get-tuple-element.3838), channel_id=1, source_target_pairs={{0,8},{8,16},{16,24},{1,9},{9,17},{17,25},{2,10},{10,18},{18,26},{... | collective-permute-start | bytes 903176 | tf_op jit(solution)/shard_map/while/body/eval_jaxpr/ppermute | solution.py:27
  228.4 39.2 %collective-permute-start = (bf16[2,14,14,384]{3,0,2,1:T(2,128)(2,1)}, bf16[2,14,14,384]{3,0,2,1:T(2,128)(2,1)}, u32[]{:S(2)}, u32[]{:S(2)}) collective-permute-start(bf16[2,14,14,384]{3,0,2,1:T(2,128)(2,1)} %get-tuple-element.3838), channel_id=1, source_target_pairs={{0,8},{8,16},{16,24},{1,9},{9,17},{17,25},{2,10},{10,18},{18,26},{... | collective-permute-start | bytes 903176 | tf_op jit(solution)/shard_map/while/body/eval_jaxpr/ppermute | solution.py:27
  299.1 51.3 %collective-permute-start = (bf16[2,14,14,384]{3,0,2,1:T(2,128)(2,1)}, bf16[2,14,14,384]{3,0,2,1:T(2,128)(2,1)}, u32[]{:S(2)}, u32[]{:S(2)}) collective-permute-start(bf16[2,14,14,384]{3,0,2,1:T(2,128)(2,1)} %get-tuple-element.3838), channel_id=1, source_target_pairs={{0,8},{8,16},{16,24},{1,9},{9,17},{17,25},{2,10},{10,18},{18,26},{... | collective-permute-start | bytes 903176 | tf_op jit(solution)/shard_map/while/body/eval_jaxpr/ppermute | solution.py:27
  301.1 49.3 %collective-permute-start.1 = (bf16[6,6,6,384]{3,2,1,0:T(8,128)(2,1)}, bf16[6,6,6,384]{3,2,1,0:T(8,128)(2,1)S(1)}, u32[]{:S(2)}, u32[]{:S(2)}) collective-permute-start(bf16[6,6,6,384]{3,2,1,0:T(8,128)(2,1)} %get-tuple-element.3839), channel_id=1, source_target_pairs={{0,8},{8,16},{16,24},{1,9},{9,17},{17,25},{2,10},{10,18},{18,26},{... | collective-permute-start | bytes 497672 | tf_op jit(solution)/shard_map/while/body/eval_jaxpr/ppermute | solution.py:27
  381.8 58.3 %collective-permute-start = (bf16[2,14,14,384]{3,0,2,1:T(2,128)(2,1)}, bf16[2,14,14,384]{3,0,2,1:T(2,128)(2,1)}, u32[]{:S(2)}, u32[]{:S(2)}) collective-permute-start(bf16[2,14,14,384]{3,0,2,1:T(2,128)(2,1)} %get-tuple-element.3838), channel_id=1, source_target_pairs={{0,8},{8,16},{16,24},{1,9},{9,17},{17,25},{2,10},{10,18},{18,26},{... | collective-permute-start | bytes 903176 | tf_op jit(solution)/shard_map/while/body/eval_jaxpr/ppermute | solution.py:27
  383.8 56.3 %collective-permute-start.1 = (bf16[6,6,6,384]{3,2,1,0:T(8,128)(2,1)}, bf16[6,6,6,384]{3,2,1,0:T(8,128)(2,1)S(1)}, u32[]{:S(2)}, u32[]{:S(2)}) collective-permute-start(bf16[6,6,6,384]{3,2,1,0:T(8,128)(2,1)} %get-tuple-element.3839), channel_id=1, source_target_pairs={{0,8},{8,16},{16,24},{1,9},{9,17},{17,25},{2,10},{10,18},{18,26},{... | collective-permute-start | bytes 497672 | tf_op jit(solution)/shard_map/while/body/eval_jaxpr/ppermute | solution.py:27
  471.6 57.6 %collective-permute-start = (bf16[2,14,14,384]{3,0,2,1:T(2,128)(2,1)}, bf16[2,14,14,384]{3,0,2,1:T(2,128)(2,1)}, u32[]{:S(2)}, u32[]{:S(2)}) collective-permute-start(bf16[2,14,14,384]{3,0,2,1:T(2,128)(2,1)} %get-tuple-element.3838), channel_id=1, source_target_pairs={{0,8},{8,16},{16,24},{1,9},{9,17},{17,25},{2,10},{10,18},{18,26},{... | collective-permute-start | bytes 903176 | tf_op jit(solution)/shard_map/while/body/eval_jaxpr/ppermute | solution.py:27
  473.6 55.6 %collective-permute-start.1 = (bf16[6,6,6,384]{3,2,1,0:T(8,128)(2,1)}, bf16[6,6,6,384]{3,2,1,0:T(8,128)(2,1)S(1)}, u32[]{:S(2)}, u32[]{:S(2)}) collective-permute-start(bf16[6,6,6,384]{3,2,1,0:T(8,128)(2,1)} %get-tuple-element.3839), channel_id=1, source_target_pairs={{0,8},{8,16},{16,24},{1,9},{9,17},{17,25},{2,10},{10,18},{18,26},{... | collective-permute-start | bytes 497672 | tf_op jit(solution)/shard_map/while/body/eval_jaxpr/ppermute | solution.py:27
  560.7 56.2 %collective-permute-start = (bf16[2,14,14,384]{3,0,2,1:T(2,128)(2,1)}, bf16[2,14,14,384]{3,0,2,1:T(2,128)(2,1)}, u32[]{:S(2)}, u32[]{:S(2)}) collective-permute-start(bf16[2,14,14,384]{3,0,2,1:T(2,128)(2,1)} %get-tuple-element.3838), channel_id=1, source_target_pairs={{0,8},{8,16},{16,24},{1,9},{9,17},{17,25},{2,10},{10,18},{18,26},{... | collective-permute-start | bytes 903176 | tf_op jit(solution)/shard_map/while/body/eval_jaxpr/ppermute | solution.py:27
  562.7 54.2 %collective-permute-start.1 = (bf16[6,6,6,384]{3,2,1,0:T(8,128)(2,1)}, bf16[6,6,6,384]{3,2,1,0:T(8,128)(2,1)S(1)}, u32[]{:S(2)}, u32[]{:S(2)}) collective-permute-start(bf16[6,6,6,384]{3,2,1,0:T(8,128)(2,1)} %get-tuple-element.3839), channel_id=1, source_target_pairs={{0,8},{8,16},{16,24},{1,9},{9,17},{17,25},{2,10},{10,18},{18,26},{... | collective-permute-start | bytes 497672 | tf_op jit(solution)/shard_map/while/body/eval_jaxpr/ppermute | solution.py:27
  648.4 54.9 %collective-permute-start = (bf16[2,14,14,384]{3,0,2,1:T(2,128)(2,1)}, bf16[2,14,14,384]{3,0,2,1:T(2,128)(2,1)}, u32[]{:S(2)}, u32[]{:S(2)}) collective-permute-start(bf16[2,14,14,384]{3,0,2,1:T(2,128)(2,1)} %get-tuple-element.3838), channel_id=1, source_target_pairs={{0,8},{8,16},{16,24},{1,9},{9,17},{17,25},{2,10},{10,18},{18,26},{... | collective-permute-start | bytes 903176 | tf_op jit(solution)/shard_map/while/body/eval_jaxpr/ppermute | solution.py:27
  650.4 52.9 %collective-permute-start.1 = (bf16[6,6,6,384]{3,2,1,0:T(8,128)(2,1)}, bf16[6,6,6,384]{3,2,1,0:T(8,128)(2,1)S(1)}, u32[]{:S(2)}, u32[]{:S(2)}) collective-permute-start(bf16[6,6,6,384]{3,2,1,0:T(8,128)(2,1)} %get-tuple-element.3839), channel_id=1, source_target_pairs={{0,8},{8,16},{16,24},{1,9},{9,17},{17,25},{2,10},{10,18},{18,26},{... | collective-permute-start | bytes 497672 | tf_op jit(solution)/shard_map/while/body/eval_jaxpr/ppermute | solution.py:27
  734.7 54.6 %collective-permute-start = (bf16[2,14,14,384]{3,0,2,1:T(2,128)(2,1)}, bf16[2,14,14,384]{3,0,2,1:T(2,128)(2,1)}, u32[]{:S(2)}, u32[]{:S(2)}) collective-permute-start(bf16[2,14,14,384]{3,0,2,1:T(2,128)(2,1)} %get-tuple-element.3838), channel_id=1, source_target_pairs={{0,8},{8,16},{16,24},{1,9},{9,17},{17,25},{2,10},{10,18},{18,26},{... | collective-permute-start | bytes 903176 | tf_op jit(solution)/shard_map/while/body/eval_jaxpr/ppermute | solution.py:27
  736.7 52.6 %collective-permute-start.1 = (bf16[6,6,6,384]{3,2,1,0:T(8,128)(2,1)}, bf16[6,6,6,384]{3,2,1,0:T(8,128)(2,1)S(1)}, u32[]{:S(2)}, u32[]{:S(2)}) collective-permute-start(bf16[6,6,6,384]{3,2,1,0:T(8,128)(2,1)} %get-tuple-element.3839), channel_id=1, source_target_pairs={{0,8},{8,16},{16,24},{1,9},{9,17},{17,25},{2,10},{10,18},{18,26},{... | collective-permute-start | bytes 497672 | tf_op jit(solution)/shard_map/while/body/eval_jaxpr/ppermute | solution.py:27
  801.1 74.2 %collective-permute-start = (bf16[2,14,14,384]{3,0,2,1:T(2,128)(2,1)}, bf16[2,14,14,384]{3,0,2,1:T(2,128)(2,1)}, u32[]{:S(2)}, u32[]{:S(2)}) collective-permute-start(bf16[2,14,14,384]{3,0,2,1:T(2,128)(2,1)} %get-tuple-element.3838), channel_id=1, source_target_pairs={{0,8},{8,16},{16,24},{1,9},{9,17},{17,25},{2,10},{10,18},{18,26},{... | collective-permute-start | bytes 903176 | tf_op jit(solution)/shard_map/while/body/eval_jaxpr/ppermute | solution.py:27
  820.9 54.5 %collective-permute-start.1 = (bf16[6,6,6,384]{3,2,1,0:T(8,128)(2,1)}, bf16[6,6,6,384]{3,2,1,0:T(8,128)(2,1)S(1)}, u32[]{:S(2)}, u32[]{:S(2)}) collective-permute-start(bf16[6,6,6,384]{3,2,1,0:T(8,128)(2,1)} %get-tuple-element.3839), channel_id=1, source_target_pairs={{0,8},{8,16},{16,24},{1,9},{9,17},{17,25},{2,10},{10,18},{18,26},{... | collective-permute-start | bytes 497672 | tf_op jit(solution)/shard_map/while/body/eval_jaxpr/ppermute | solution.py:27
  887.1 74.2 %collective-permute-start = (bf16[2,14,14,384]{3,0,2,1:T(2,128)(2,1)}, bf16[2,14,14,384]{3,0,2,1:T(2,128)(2,1)}, u32[]{:S(2)}, u32[]{:S(2)}) collective-permute-start(bf16[2,14,14,384]{3,0,2,1:T(2,128)(2,1)} %get-tuple-element.3838), channel_id=1, source_target_pairs={{0,8},{8,16},{16,24},{1,9},{9,17},{17,25},{2,10},{10,18},{18,26},{... | collective-permute-start | bytes 903176 | tf_op jit(solution)/shard_map/while/body/eval_jaxpr/ppermute | solution.py:27
  893.0 68.4 %collective-permute-start.1 = (bf16[6,6,6,384]{3,2,1,0:T(8,128)(2,1)}, bf16[6,6,6,384]{3,2,1,0:T(8,128)(2,1)S(1)}, u32[]{:S(2)}, u32[]{:S(2)}) collective-permute-start(bf16[6,6,6,384]{3,2,1,0:T(8,128)(2,1)} %get-tuple-element.3839), channel_id=1, source_target_pairs={{0,8},{8,16},{16,24},{1,9},{9,17},{17,25},{2,10},{10,18},{18,26},{... | collective-permute-start | bytes 497672 | tf_op jit(solution)/shard_map/while/body/eval_jaxpr/ppermute | solution.py:27
  973.2 42.0 %collective-permute-start = (bf16[2,14,14,384]{3,0,2,1:T(2,128)(2,1)}, bf16[2,14,14,384]{3,0,2,1:T(2,128)(2,1)}, u32[]{:S(2)}, u32[]{:S(2)}) collective-permute-start(bf16[2,14,14,384]{3,0,2,1:T(2,128)(2,1)} %get-tuple-element.3838), channel_id=1, source_target_pairs={{0,8},{8,16},{16,24},{1,9},{9,17},{17,25},{2,10},{10,18},{18,26},{... | collective-permute-start | bytes 903176 | tf_op jit(solution)/shard_map/while/body/eval_jaxpr/ppermute | solution.py:27
  1016.5 1470.9 %reduce-scatter.4.cloned.1.call-start = ((), (), s32[]{:S(2)}) async-start(), calls=%async_computation.6 | async-start | bytes 2211840 | tf_op jit(solution)/shard_map/reduce_scatter | solution.py:542
  1021.9 1614.4 %all-reduce.7.cloned.1.call-start = ((), (), s32[]{:S(2)}) async-start(), calls=%async_computation.10 | async-start | bytes 19267584 | tf_op jit(solution)/shard_map/psum | solution.py:547
  1076.8 43.3 %collective-permute-start.6 = (f32[2,14,14,384]{3,0,2,1:T(2,128)}, f32[2,14,14,384]{3,0,2,1:T(2,128)}, u32[]{:S(2)}, u32[]{:S(2)}) collective-permute-start(f32[2,14,14,384]{3,0,2,1:T(2,128)} %copy.506), channel_id=1, source_target_pairs={{8,0},{16,8},{24,16},{9,1},{17,9},{25,17},{10,2},{18,10},{26,18},{... | collective-permute-start | bytes 1806344 | tf_op jit(solution)/shard_map/while/body/eval_jaxpr/ppermute | solution.py:27
  1078.1 42.0 %collective-permute-start.7 = (f32[6,6,6,384]{3,2,1,0:T(8,128)}, f32[6,6,6,384]{3,2,1,0:T(8,128)}, u32[]{:S(2)}, u32[]{:S(2)}) collective-permute-start(f32[6,6,6,384]{3,2,1,0:T(8,128)} %get-tuple-element.3886), channel_id=1, source_target_pairs={{8,0},{16,8},{24,16},{9,1},{17,9},{25,17},{10,2},{18,10},{26,18},{... | collective-permute-start | bytes 995336 | tf_op jit(solution)/shard_map/while/body/eval_jaxpr/ppermute | solution.py:27
  1213.2 157.4 %collective-permute-start.4 = (bf16[2,14,14,384]{3,0,2,1:T(2,128)(2,1)}, bf16[2,14,14,384]{3,0,2,1:T(2,128)(2,1)S(1)}, u32[]{:S(2)}, u32[]{:S(2)}) collective-permute-start(bf16[2,14,14,384]{3,0,2,1:T(2,128)(2,1)} %get-tuple-element.3883), channel_id=1, source_target_pairs={{8,0},{16,8},{24,16},{9,1},{17,9},{25,17},{10,2},{18,10},{26,18},{... | collective-permute-start | bytes 903176 | tf_op jit(solution)/shard_map/while/body/eval_jaxpr/ppermute | solution.py:27
  1214.5 156.1 %collective-permute-start.5 = (bf16[6,6,6,384]{3,2,1,0:T(8,128)(2,1)}, bf16[6,6,6,384]{3,2,1,0:T(8,128)(2,1)S(1)}, u32[]{:S(2)}, u32[]{:S(2)}) collective-permute-start(bf16[6,6,6,384]{3,2,1,0:T(8,128)(2,1)} %get-tuple-element.3884), channel_id=1, source_target_pairs={{8,0},{16,8},{24,16},{9,1},{17,9},{25,17},{10,2},{18,10},{26,18},{... | collective-permute-start | bytes 497672 | tf_op jit(solution)/shard_map/while/body/eval_jaxpr/ppermute | solution.py:27
  1218.2 166.5 %collective-permute-start.6 = (f32[2,14,14,384]{3,0,2,1:T(2,128)}, f32[2,14,14,384]{3,0,2,1:T(2,128)}, u32[]{:S(2)}, u32[]{:S(2)}) collective-permute-start(f32[2,14,14,384]{3,0,2,1:T(2,128)} %copy.506), channel_id=1, source_target_pairs={{8,0},{16,8},{24,16},{9,1},{17,9},{25,17},{10,2},{18,10},{26,18},{... | collective-permute-start | bytes 1806344 | tf_op jit(solution)/shard_map/while/body/eval_jaxpr/ppermute | solution.py:27
  1219.5 165.2 %collective-permute-start.7 = (f32[6,6,6,384]{3,2,1,0:T(8,128)}, f32[6,6,6,384]{3,2,1,0:T(8,128)}, u32[]{:S(2)}, u32[]{:S(2)}) collective-permute-start(f32[6,6,6,384]{3,2,1,0:T(8,128)} %get-tuple-element.3886), channel_id=1, source_target_pairs={{8,0},{16,8},{24,16},{9,1},{17,9},{25,17},{10,2},{18,10},{26,18},{... | collective-permute-start | bytes 995336 | tf_op jit(solution)/shard_map/while/body/eval_jaxpr/ppermute | solution.py:27
  1468.6 47.4 %collective-permute-start.6 = (f32[2,14,14,384]{3,0,2,1:T(2,128)}, f32[2,14,14,384]{3,0,2,1:T(2,128)}, u32[]{:S(2)}, u32[]{:S(2)}) collective-permute-start(f32[2,14,14,384]{3,0,2,1:T(2,128)} %copy.506), channel_id=1, source_target_pairs={{8,0},{16,8},{24,16},{9,1},{17,9},{25,17},{10,2},{18,10},{26,18},{... | collective-permute-start | bytes 1806344 | tf_op jit(solution)/shard_map/while/body/eval_jaxpr/ppermute | solution.py:27
  1469.9 46.2 %collective-permute-start.7 = (f32[6,6,6,384]{3,2,1,0:T(8,128)}, f32[6,6,6,384]{3,2,1,0:T(8,128)}, u32[]{:S(2)}, u32[]{:S(2)}) collective-permute-start(f32[6,6,6,384]{3,2,1,0:T(8,128)} %get-tuple-element.3886), channel_id=1, source_target_pairs={{8,0},{16,8},{24,16},{9,1},{17,9},{25,17},{10,2},{18,10},{26,18},{... | collective-permute-start | bytes 995336 | tf_op jit(solution)/shard_map/while/body/eval_jaxpr/ppermute | solution.py:27
  1600.0 46.2 %collective-permute-start.6 = (f32[2,14,14,384]{3,0,2,1:T(2,128)}, f32[2,14,14,384]{3,0,2,1:T(2,128)}, u32[]{:S(2)}, u32[]{:S(2)}) collective-permute-start(f32[2,14,14,384]{3,0,2,1:T(2,128)} %copy.506), channel_id=1, source_target_pairs={{8,0},{16,8},{24,16},{9,1},{17,9},{25,17},{10,2},{18,10},{26,18},{... | collective-permute-start | bytes 1806344 | tf_op jit(solution)/shard_map/while/body/eval_jaxpr/ppermute | solution.py:27
  1601.3 44.9 %collective-permute-start.7 = (f32[6,6,6,384]{3,2,1,0:T(8,128)}, f32[6,6,6,384]{3,2,1,0:T(8,128)}, u32[]{:S(2)}, u32[]{:S(2)}) collective-permute-start(f32[6,6,6,384]{3,2,1,0:T(8,128)} %get-tuple-element.3886), channel_id=1, source_target_pairs={{8,0},{16,8},{24,16},{9,1},{17,9},{25,17},{10,2},{18,10},{26,18},{... | collective-permute-start | bytes 995336 | tf_op jit(solution)/shard_map/while/body/eval_jaxpr/ppermute | solution.py:27
  1730.3 46.6 %collective-permute-start.6 = (f32[2,14,14,384]{3,0,2,1:T(2,128)}, f32[2,14,14,384]{3,0,2,1:T(2,128)}, u32[]{:S(2)}, u32[]{:S(2)}) collective-permute-start(f32[2,14,14,384]{3,0,2,1:T(2,128)} %copy.506), channel_id=1, source_target_pairs={{8,0},{16,8},{24,16},{9,1},{17,9},{25,17},{10,2},{18,10},{26,18},{... | collective-permute-start | bytes 1806344 | tf_op jit(solution)/shard_map/while/body/eval_jaxpr/ppermute | solution.py:27
  1731.6 45.3 %collective-permute-start.7 = (f32[6,6,6,384]{3,2,1,0:T(8,128)}, f32[6,6,6,384]{3,2,1,0:T(8,128)}, u32[]{:S(2)}, u32[]{:S(2)}) collective-permute-start(f32[6,6,6,384]{3,2,1,0:T(8,128)} %get-tuple-element.3886), channel_id=1, source_target_pairs={{8,0},{16,8},{24,16},{9,1},{17,9},{25,17},{10,2},{18,10},{26,18},{... | collective-permute-start | bytes 995336 | tf_op jit(solution)/shard_map/while/body/eval_jaxpr/ppermute | solution.py:27
  1855.8 38.7 %collective-permute-start.4 = (bf16[2,14,14,384]{3,0,2,1:T(2,128)(2,1)}, bf16[2,14,14,384]{3,0,2,1:T(2,128)(2,1)S(1)}, u32[]{:S(2)}, u32[]{:S(2)}) collective-permute-start(bf16[2,14,14,384]{3,0,2,1:T(2,128)(2,1)} %get-tuple-element.3883), channel_id=1, source_target_pairs={{8,0},{16,8},{24,16},{9,1},{17,9},{25,17},{10,2},{18,10},{26,18},{... | collective-permute-start | bytes 903176 | tf_op jit(solution)/shard_map/while/body/eval_jaxpr/ppermute | solution.py:27
  1860.8 46.7 %collective-permute-start.6 = (f32[2,14,14,384]{3,0,2,1:T(2,128)}, f32[2,14,14,384]{3,0,2,1:T(2,128)}, u32[]{:S(2)}, u32[]{:S(2)}) collective-permute-start(f32[2,14,14,384]{3,0,2,1:T(2,128)} %copy.506), channel_id=1, source_target_pairs={{8,0},{16,8},{24,16},{9,1},{17,9},{25,17},{10,2},{18,10},{26,18},{... | collective-permute-start | bytes 1806344 | tf_op jit(solution)/shard_map/while/body/eval_jaxpr/ppermute | solution.py:27
  1862.1 45.4 %collective-permute-start.7 = (f32[6,6,6,384]{3,2,1,0:T(8,128)}, f32[6,6,6,384]{3,2,1,0:T(8,128)}, u32[]{:S(2)}, u32[]{:S(2)}) collective-permute-start(f32[6,6,6,384]{3,2,1,0:T(8,128)} %get-tuple-element.3886), channel_id=1, source_target_pairs={{8,0},{16,8},{24,16},{9,1},{17,9},{25,17},{10,2},{18,10},{26,18},{... | collective-permute-start | bytes 995336 | tf_op jit(solution)/shard_map/while/body/eval_jaxpr/ppermute | solution.py:27
  1991.4 45.3 %collective-permute-start.6 = (f32[2,14,14,384]{3,0,2,1:T(2,128)}, f32[2,14,14,384]{3,0,2,1:T(2,128)}, u32[]{:S(2)}, u32[]{:S(2)}) collective-permute-start(f32[2,14,14,384]{3,0,2,1:T(2,128)} %copy.506), channel_id=1, source_target_pairs={{8,0},{16,8},{24,16},{9,1},{17,9},{25,17},{10,2},{18,10},{26,18},{... | collective-permute-start | bytes 1806344 | tf_op jit(solution)/shard_map/while/body/eval_jaxpr/ppermute | solution.py:27
  1992.7 44.0 %collective-permute-start.7 = (f32[6,6,6,384]{3,2,1,0:T(8,128)}, f32[6,6,6,384]{3,2,1,0:T(8,128)}, u32[]{:S(2)}, u32[]{:S(2)}) collective-permute-start(f32[6,6,6,384]{3,2,1,0:T(8,128)} %get-tuple-element.3886), channel_id=1, source_target_pairs={{8,0},{16,8},{24,16},{9,1},{17,9},{25,17},{10,2},{18,10},{26,18},{... | collective-permute-start | bytes 995336 | tf_op jit(solution)/shard_map/while/body/eval_jaxpr/ppermute | solution.py:27
  2120.8 45.7 %collective-permute-start.6 = (f32[2,14,14,384]{3,0,2,1:T(2,128)}, f32[2,14,14,384]{3,0,2,1:T(2,128)}, u32[]{:S(2)}, u32[]{:S(2)}) collective-permute-start(f32[2,14,14,384]{3,0,2,1:T(2,128)} %copy.506), channel_id=1, source_target_pairs={{8,0},{16,8},{24,16},{9,1},{17,9},{25,17},{10,2},{18,10},{26,18},{... | collective-permute-start | bytes 1806344 | tf_op jit(solution)/shard_map/while/body/eval_jaxpr/ppermute | solution.py:27
  2122.1 44.4 %collective-permute-start.7 = (f32[6,6,6,384]{3,2,1,0:T(8,128)}, f32[6,6,6,384]{3,2,1,0:T(8,128)}, u32[]{:S(2)}, u32[]{:S(2)}) collective-permute-start(f32[6,6,6,384]{3,2,1,0:T(8,128)} %get-tuple-element.3886), channel_id=1, source_target_pairs={{8,0},{16,8},{24,16},{9,1},{17,9},{25,17},{10,2},{18,10},{26,18},{... | collective-permute-start | bytes 995336 | tf_op jit(solution)/shard_map/while/body/eval_jaxpr/ppermute | solution.py:27
  2250.4 45.8 %collective-permute-start.6 = (f32[2,14,14,384]{3,0,2,1:T(2,128)}, f32[2,14,14,384]{3,0,2,1:T(2,128)}, u32[]{:S(2)}, u32[]{:S(2)}) collective-permute-start(f32[2,14,14,384]{3,0,2,1:T(2,128)} %copy.506), channel_id=1, source_target_pairs={{8,0},{16,8},{24,16},{9,1},{17,9},{25,17},{10,2},{18,10},{26,18},{... | collective-permute-start | bytes 1806344 | tf_op jit(solution)/shard_map/while/body/eval_jaxpr/ppermute | solution.py:27
  2251.7 44.5 %collective-permute-start.7 = (f32[6,6,6,384]{3,2,1,0:T(8,128)}, f32[6,6,6,384]{3,2,1,0:T(8,128)}, u32[]{:S(2)}, u32[]{:S(2)}) collective-permute-start(f32[6,6,6,384]{3,2,1,0:T(8,128)} %get-tuple-element.3886), channel_id=1, source_target_pairs={{8,0},{16,8},{24,16},{9,1},{17,9},{25,17},{10,2},{18,10},{26,18},{... | collective-permute-start | bytes 995336 | tf_op jit(solution)/shard_map/while/body/eval_jaxpr/ppermute | solution.py:27
  2409.1 277.8 %reduce-scatter.8.cloned.1.call-start = ((), (), s32[]{:S(2)}) async-start(), calls=%async_computation.8 | async-start | bytes 4423680 | tf_op jit(solution)/shard_map/reduce_scatter | solution.py:544
  2409.8 344.0 %reduce-scatter.6.cloned.1.call-start = ((), (), s32[]{:S(2)}) async-start(), calls=%async_computation.7 | async-start | bytes 6881280 | tf_op jit(solution)/shard_map/reduce_scatter | solution.py:543
  (349 other events, 7952.5 us)
Sparse Core Ops, SparseCore 0:
  10.2 25.8 all-gather.4
  38.4 22.3 all-gather.6
  63.0 31.3 all-gather.8
  1016.1 91.0 all-reduce.4
  1110.3 44.6 reduce-scatter.3
  2409.2 227.1 all-reduce.6
  2639.7 47.0 reduce-scatter.7
  2690.2 63.5 reduce-scatter.5
where the time goes:
time: 2800 us; the launch traced here: 2760 us
  waiting for transfers between devices  890 us (32%)
  local copies, waits for them, and re-layouts  591 us (21%)
  starting transfers between devices  380 us (14%)
  matrix products  290 us (10%)
  other arithmetic  277 us (10%)
  loops' own time  218 us (8%)
  blocking collectives  103 us (4%)
    ppermute x88, waiting for transfers between devices, shifted(): return lax.ppermute(shard, axis, pairs)  593 us
    ppermute x88, starting transfers between devices, shifted(): return lax.ppermute(shard, axis, pairs)  380 us
    conv_general_dilated x64, matrix products, depthwise(): lax.conv_general_dilated(crop_field, kernel.reshape(KS, KS, 1, channels),...  290 us
    another operation x11, loops' own time, behind(): lax.switch(jnp.where(is_active, section_rank, sections), backward_list +...  168 us
    psum x1, waiting for transfers between devices, body(): lax.psum((totals[0], totals[1], totals[2], totals[3], totals[4]), ('secti...  147 us
    another operation x60, local copies, waits for them, and re-layouts  139 us
    dynamic_slice x88, local copies, waits for them, and re-layouts, take_slot(): return lax.dynamic_index_in_dim(buffer, slot_index, 0, keepdims=False)  104 us
    dynamic_update_slice x66, other arithmetic, put_slot(): lax.dynamic_update_index_in_dim(buffer, jnp.where(is_active, entry_value,...  94.2 us
  transfers between devices with their start and end apart: 96, of which 38 were waited for; matrix products, arithmetic and copies ran while one was open for 31% of the time, Pallas kernels for 0%

commit v1 on v0

v1 whole, which is shorter than its diff:
```python
import math

import jax
import jax.numpy as jnp
from jax import lax
from jax.experimental import pallas as pl
from jax.experimental.pallas import tpu as pltpu
from jax.sharding import PartitionSpec as P

C = 384
FF = 1536
C2 = 768
KS = 7
BIG_IMG = 2
SMALL_IMG = 6

KEEP_RATE = 0.9
MOMENTUM = 0.5
AVERAGING = 0.5
EPSILON = 1e-06
RATES = (1.1, 0.4, 2.7, 1.3, 1.3)
FANS = (KS * KS, 1, C, FF, 4 * C)
UP_ROWS = FF // C


def layer_norm(values, gain_row, offset_row):
    average = jnp.mean(values, axis=-1, keepdims=True)
    centered = values - average
    variance = jnp.mean(centered * centered, axis=-1, keepdims=True)
    return centered * lax.rsqrt(variance + EPSILON) * gain_row + offset_row


def depthwise(field, kernel, precision):
    radius = KS // 2
    channels = field.shape[-1]
    return lax.conv_general_dilated(
        field,
        kernel.reshape(KS, KS, 1, channels),
        (1, 1),
        ((radius, radius), (radius, radius)),
        dimension_numbers=("NHWC", "HWIO", "NHWC"),
        feature_group_count=channels,
        precision=precision,
        preferred_element_type=jnp.float32,
    )


def to_blocks(field):
    count, side = field.shape[0], field.shape[1]
    half = side // 2
    return (
        field.reshape(count, half, 2, half, 2, C)
        .transpose(0, 1, 3, 2, 4, 5)
        .reshape(count * half * half, 4 * C)
    )


def from_blocks(flat, shape):
    count, half = shape[0], shape[1] // 2
    return flat.reshape(count, half, half, 2, 2, C).transpose(0, 1, 3, 2, 4, 5).reshape(shape)


def contract(left, right):
    return lax.dot_general(left, right, (((0,), (0,)), ((), ())), preferred_element_type=jnp.float32)


def dot_t(left, right):
    return lax.dot_general(left, right, (((1,), (1,)), ((), ())), preferred_element_type=jnp.float32)


def group_step(crops, cot, keep, kernel, values, up, down, strided):
    bias_dw, gain_one, offset_one = values[0], values[1], values[2]
    bias_up = values[3 : 3 + UP_ROWS].reshape(FF)
    bias_down, layer_scale = values[3 + UP_ROWS], values[4 + UP_ROWS]
    gain_two, offset_two = values[5 + UP_ROWS], values[6 + UP_ROWS]
    bias_out = values[7 + UP_ROWS :].reshape(C2)
    up_scale, down_scale, strided_scale = 1 / math.sqrt(C), 1 / math.sqrt(FF), 1 / math.sqrt(4 * C)
    side = crops.shape[1]
    factor = jnp.repeat(keep, side * side)[:, None]
    field = crops.astype(jnp.float32)

    def first(field_value, kernel_value, bias, gain, offset):
        conv_out = depthwise(field_value, kernel_value, None) * (1.0 / KS) + bias
        return layer_norm(conv_out, gain, offset)

    normed, first_pull = jax.vjp(first, field, kernel.astype(jnp.float32), bias_dw, gain_one, offset_one)
    rows = normed.astype(jnp.bfloat16).reshape(-1, C)
    pre_act = jnp.dot(rows, up, preferred_element_type=jnp.float32) * up_scale + bias_up
    phi_big = 0.5 * (1.0 + lax.erf(pre_act * math.sqrt(0.5)))
    density = jnp.exp(-0.5 * pre_act * pre_act) * (1.0 / math.sqrt(2.0 * math.pi))
    slope = phi_big + pre_act * density
    hidden = (pre_act * phi_big).astype(jnp.bfloat16)
    branch = jnp.dot(hidden, down, preferred_element_type=jnp.float32) * down_scale + bias_down
    mixed = field.reshape(-1, C) + layer_scale * branch * factor
    zeta, norm_pull = jax.vjp(layer_norm, mixed, gain_two, offset_two)
    blocks = to_blocks(zeta.astype(jnp.bfloat16).reshape(crops.shape))
    result = jnp.dot(blocks, strided, preferred_element_type=jnp.float32) * strided_scale + bias_out

    grad_out = cot.reshape(-1, C2)
    d_strided = contract(blocks, grad_out) * strided_scale
    d_bias_out = jnp.sum(grad_out.astype(jnp.float32), axis=0)
    d_blocks = dot_t(grad_out, strided) * strided_scale
    d_zeta = from_blocks(d_blocks.astype(jnp.bfloat16), crops.shape).reshape(-1, C)
    d_mixed, d_gain_two, d_offset_two = norm_pull(d_zeta.astype(jnp.float32))
    d_scale = jnp.sum(d_mixed * factor * branch, axis=0)
    d_branch = (d_mixed * factor * layer_scale).astype(jnp.bfloat16)
    d_bias_down = jnp.sum(d_branch.astype(jnp.float32), axis=0)
    d_down = contract(hidden, d_branch) * down_scale
    d_pre = (dot_t(d_branch, down) * down_scale * slope).astype(jnp.bfloat16)
    d_bias_up = jnp.sum(d_pre.astype(jnp.float32), axis=0)
    d_up = contract(rows, d_pre) * up_scale
    d_normed = (dot_t(d_pre, up) * up_scale).astype(jnp.bfloat16).reshape(crops.shape)
    d_field, d_kernel, d_bias_dw, d_gain_one, d_offset_one = first_pull(d_normed.astype(jnp.float32))
    d_vector = jnp.concatenate(
        [
            d_bias_dw[None],
            d_gain_one[None],
            d_offset_one[None],
            d_bias_up.reshape(UP_ROWS, C),
            d_bias_down[None],
            d_scale[None],
            d_gain_two[None],
            d_offset_two[None],
            d_bias_out.reshape(C2 // C, C),
        ]
    )
    half = side // 2
    return (
        result.reshape(-1, half, half, C2),
        d_field + d_mixed.reshape(crops.shape),
        (d_kernel, d_vector, d_up, d_down, d_strided),
    )


def plain_body(big_crops, small_crops, big_cot, small_cot, drop_mask, *state):
    masters, moments, averages = state[0::3], state[1::3], state[2::3]
    axes = (1, 1, 1, 0, 0)
    full = [
        lax.all_gather(weight.astype(jnp.bfloat16), "dp", axis=axis, tiled=True)
        for weight, axis in zip(masters, axes)
    ]
    kernel, vector, up, down, strided = full
    values = vector.astype(jnp.float32)
    sections, rank = lax.axis_size("section"), lax.axis_index("section")
    micro_count = big_crops.shape[0]
    own = micro_count // sections

    def take(array):
        return lax.dynamic_slice_in_dim(array, rank * own, own, 0)

    keep = take(drop_mask).astype(jnp.float32) / KEEP_RATE
    outputs, grads, totals = [], [], None
    for crops, cot, images in ((big_crops, big_cot, BIG_IMG), (small_crops, small_cot, SMALL_IMG)):
        mine, my_cot = take(crops), take(cot)
        result, grad, parts = group_step(
            mine.reshape(-1, *crops.shape[2:]),
            my_cot.reshape(-1, *cot.shape[2:]),
            jnp.repeat(keep, images, axis=1).reshape(-1),
            kernel,
            values,
            up,
            down,
            strided,
        )
        outputs.append(result.reshape(my_cot.shape))
        grads.append(grad.reshape(mine.shape))
        totals = parts if totals is None else [a + b for a, b in zip(totals, parts)]
    pixel_total = (
        lax.axis_size("dp")
        * micro_count
        * (math.prod(big_crops.shape[1:4]) + math.prod(small_crops.shape[1:4]))
    )
    updates = []
    for position in range(5):
        gradient = lax.psum_scatter(totals[position], "dp", scatter_dimension=axes[position], tiled=True)
        gradient = lax.psum(gradient, "section")
        step_rate = RATES[position] * math.sqrt(FANS[position] / pixel_total)
        moment_next = MOMENTUM * moments[position] + gradient
        weight_next = masters[position] - step_rate * (gradient + MOMENTUM * moment_next)
        average_next = AVERAGING * averages[position] + (1.0 - AVERAGING) * weight_next
        updates += [weight_next, moment_next, average_next]
    return (*outputs, *grads, *updates)


UNIT = 4
MESH = pl.DeviceIdType.MESH
F32, BF16 = jnp.float32, jnp.bfloat16
BIG_SIDE, SMALL_SIDE = 14, 6
BIG_HALF, SMALL_HALF = 7, 3
BIG_ROWS = BIG_HALF * BIG_SIDE * 8
SMALL_ROWS = SMALL_HALF * SMALL_SIDE * 8
UNITS = 3
ROWS = BIG_ROWS + UNITS * SMALL_ROWS
HALO_BIG = (BIG_HALF + 6) * BIG_SIDE * 8
HALO_SMALL = (SMALL_HALF + 6) * SMALL_SIDE * 8
BLOCK_BIG = 7 * 32
BLOCKS = BLOCK_BIG + UNITS * 3 * 16
TILE = 304
CHUNK = C
PIECE = 48
PLANES = 4
UP_SCALE, DOWN_SCALE, STRIDED_SCALE = 1 / math.sqrt(C), 1 / math.sqrt(FF), 1 / math.sqrt(4 * C)
TAPS = KS * KS
V_BIAS_DW, V_GAIN_ONE, V_OFFSET_ONE, V_BIAS_UP = 0, 1, 2, 3
V_BIAS_DOWN, V_SCALE, V_GAIN_TWO, V_OFFSET_TWO, V_BIAS_OUT = 7, 8, 9, 10, 11


def nn(a, b):
    return jnp.dot(a, b, preferred_element_type=F32)


def rows_at(start, size):
    return pl.ds(pl.multiple_of(start, 8), size)


def one_hot(shape, target, valid=None):
    row = lax.broadcasted_iota(jnp.int32, shape, 0)
    column = lax.broadcasted_iota(jnp.int32, shape, 1)
    hit = column == target(row)
    if valid is not None:
        hit = hit & valid(row)
    return jnp.where(hit, 1.0, 0.0).astype(BF16)


def flat(value):
    return value.reshape(-1, value.shape[-1])


def step_kernel(
    big_hbm, small_hbm, big_cot_hbm, small_cot_hbm, keep_ref, kernel_ref, vector_ref, up_shard, down_shard, strided_shard,
    out_big_ref, out_small_ref, grad_big_ref, grad_small_ref, kv_out, up_out, down_out, strided_out,
    xb_raw, xs_raw, gb_raw, gs_raw, halo_big, halo_small, taps, vec, conv, rstd_one, normed,
    hidden, slope, branch, xhat, rstd_two, zeta, blocks, g_wide, g_rows, d_zeta, d_mixed, d_branch, d_pre, d_normed,
    dhalo_big, dhalo_small, d_taps, d_vec, d_bias_up,
    kv_all, up_all, down_all, strided_all, d_up, d_down, d_strided,
    up_core, down_core, strided_core, up_plane, down_plane, strided_plane, up_line, down_line, strided_line,
    up_sum, down_sum, strided_sum, d_kv, kv_core, kv_plane, kv_line, kv_sum, kv_turn,
    sems, send_sems, recv_sems,
):
    pad_big = branch.at[0:896]
    rank, dp_rank = lax.axis_index("section"), lax.axis_index("dp")
    line, core = dp_rank // 2, lax.rem(dp_rank, 2)
    flanks = (rank + 1 - 2 * lax.rem(rank, 2), rank + 2 - 4 * (rank // 2), 3 - rank)
    twin = {"section": rank, "dp": dp_rank + 1 - 2 * core}

    def ahead(offset):
        return lax.rem(line + offset, PLANES)

    def on_line(offset):
        return {"section": rank, "dp": ahead(offset) * 2 + core}

    def on_plane(index):
        return {"section": flanks[index], "dp": dp_rank}

    barrier = pltpu.get_barrier_semaphore()
    for target in [twin] + [on_plane(index) for index in range(3)] + [on_line(offset) for offset in (1, 2, 3)]:
        pl.semaphore_signal(barrier, inc=1, device_id=target, device_id_type=MESH)

    pending = []

    def send(source, target_ref, target):
        index = len(pending)
        copy = pltpu.make_async_remote_copy(
            source, target_ref, send_sems.at[index], recv_sems.at[index], device_id=target, device_id_type=MESH
        )
        copy.start()
        pending.append(copy)
        return copy

    def arrived(copies):
        for copy in copies:
            copy.wait_recv()

    def piece(index):
        return pl.ds(pl.multiple_of(index * PIECE, 16), PIECE)

    def gather_line(ref, whole=False):
        part = ref.at[line, core] if whole else ref.at[line, core, piece(rank)]
        return [send(part, part, on_line(offset)) for offset in (1, 2, 3)]

    def gather_plane(ref, copies):
        result = []
        for offset, copy in zip((1, 2, 3), copies):
            copy.wait_recv()
            part = ref.at[ahead(PLANES - offset), core, piece(rank)]
            result += [send(part, part, on_plane(index)) for index in range(3)]
        return result

    def gather_core(ref, copies):
        arrived(copies)
        part = ref.at[:, core]
        return [send(part, part, twin)]

    def reduce_core(partial, landing):
        return [send(partial.at[:, 1 - core], landing, twin)]

    def reduce_plane(partial, landing, plane, copies):
        arrived(copies)
        for index in range(PLANES):
            landing[index] = (landing[index].astype(F32) + partial[index, core].astype(F32)).astype(BF16)
        return [
            send(landing.at[:, piece(flanks[index])], plane.at[index], on_plane(index)) for index in range(3)
        ]

    def reduce_line(landing, plane, ways, copies):
        arrived(copies)
        result = []
        for offset in (1, 2, 3, 0):
            index = ahead(offset)
            total = landing[index, piece(rank)].astype(F32)
            for source in range(3):
                total = total + plane[source, index].astype(F32)
            if offset:
                ways[offset - 1] = total.astype(BF16)
                result.append(send(ways.at[offset - 1], ways.at[2 + offset], on_line(offset)))
            else:
                ways[6] = total.astype(BF16)
        return result

    def reduce_back(ways, final, copies):
        arrived(copies)
        total = ways[6].astype(F32)
        for offset in (1, 2, 3):
            total = total + ways[2 + offset].astype(F32)
        final[piece(rank), :] = total.astype(BF16)
        part = final.at[piece(rank)]
        return [send(part, part, on_plane(index)) for index in range(3)]

    up_all[line, core] = up_shard[...].astype(BF16)
    down_all[line, core] = down_shard[...].astype(BF16)
    strided_all[line, core] = strided_shard[...].astype(BF16)
    put_taps = one_hot((TAPS, 128), lambda r: r)
    put_vector = one_hot((13, 128), lambda r: r + 64)
    kv_all[line, core] = (
        nn(kernel_ref[...].astype(BF16), put_taps)
        + lax.dot_general(
            vector_ref[...].astype(BF16), put_vector, (((0,), (0,)), ((), ())), preferred_element_type=F32
        )
    ).astype(BF16)
    pl.semaphore_wait(barrier, 7)
    kv_way = gather_line(kv_all, True)
    up_way = gather_line(up_all)
    down_way = gather_line(down_all)
    strided_way = gather_line(strided_all)

    own = pl.ds(rank * 2, 2)
    copies = [
        pltpu.make_async_copy(source, target, sems.at[index])
        for index, (source, target) in enumerate(
            (
                (big_hbm.at[own], xb_raw),
                (small_hbm, xs_raw),
                (big_cot_hbm.at[own], gb_raw),
                (small_cot_hbm, gs_raw),
            )
        )
    ]
    for copy in copies:
        copy.start()

    spread_big = one_hot((112, 128), lambda r: ((r >> 1) & 3) * 32 + (r >> 3) * 2 + (r & 1))
    spread_small = one_hot((48, 192), lambda r: ((r >> 1) & 3) * 48 + (r >> 3) * 8 + 2 * rank + (r & 1))
    gather_big = one_hot((128, 112), lambda r: ((r >> 1) & 15) * 8 + (r >> 5) * 2 + (r & 1))
    gather_small = one_hot((64, 48), lambda r: ((r >> 1) & 7) * 8 + (r >> 4) * 2 + (r & 1))
    block_big = one_hot(
        (128, 112), lambda r: (((r >> 1) & 7) * 2 + ((r >> 5) & 1)) * 8 + (r >> 6) * 4 + ((r >> 4) & 1) * 2 + (r & 1)
    )
    block_small = one_hot(
        (64, 48), lambda r: (((r >> 1) & 3) * 2 + ((r >> 4) & 1)) * 8 + (r >> 5) * 4 + ((r >> 3) & 1) * 2 + (r & 1)
    )
    pick_small = one_hot(
        (16, 48), lambda r: (r >> 3) * 24 + ((r >> 1) & 3) * 8 + 2 * rank + (r & 1), lambda r: (r & 7) < 6
    )
    sub = lax.broadcasted_iota(jnp.int32, (8, 128), 0)
    top = jnp.where(sub < 4, 1.0, 0.0).astype(F32)
    bottom = 1.0 - top

    def vector_row(index):
        return vec[index : index + 1, :]

    keep_zero = keep_ref[0, 0].astype(F32) / KEEP_RATE
    keep_one = keep_ref[1, 0].astype(F32) / KEEP_RATE
    lane_wide = lambda value: jnp.concatenate([value] * 3, axis=1)
    big_factor = lane_wide(jnp.where((sub & 2) == 0, keep_zero, keep_one))
    small_factor = lane_wide(jnp.where((sub & 1) == 0, keep_zero, keep_one))

    pad_big[...] = jnp.zeros_like(pad_big)
    g_wide[...] = jnp.zeros_like(g_wide)

    for copy in copies:
        copy.wait()

    for micro in range(2):
        def put_big(h, _):
            pad_big[rows_at((micro * 14 + h) * 32, 28), :] = xb_raw[micro, h].astype(F32).reshape(28, C)
            return 0

        lax.fori_loop(0, 14, put_big, 0)
        for p in range(7):
            start = p * 32 + micro * 16
            g_wide[start : start + 14, :] = gb_raw[micro, p].astype(F32).reshape(14, C2)
    for unit in range(UNITS):
        for p in range(3):
            source = jnp.concatenate(
                [gs_raw[2 * unit + crop, p].astype(F32).reshape(24, C2) for crop in range(2)], axis=0
            )
            start = BLOCK_BIG + (unit * 3 + p) * 16
            g_wide[start : start + 16, :] = nn(pick_small, source.astype(BF16))

    def spread_rows(hh, _):
        tiles = [pad_big[rows_at((micro * 14 + half * 7 + hh) * 32, 32), :] for half in range(2) for micro in range(2)]
        source = jnp.concatenate(tiles, axis=0).astype(BF16)
        halo_big[rows_at((hh + 3) * 112, 112), :] = nn(spread_big, source)
        return 0

    lax.fori_loop(0, BIG_HALF, spread_rows, 0)
    for unit in range(UNITS):
        def spread_unit(hh, _):
            tiles = [
                xs_raw[2 * unit + crop, half * 3 + hh].reshape(48, C) for half in range(2) for crop in range(2)
            ]
            source = jnp.concatenate(tiles, axis=0)
            halo_small[rows_at(unit * HALO_SMALL + (hh + 3) * 48, 48), :] = nn(spread_small, source)
            return 0

        lax.fori_loop(0, SMALL_HALF, spread_unit, 0)

    def halos(ref, base, half, side):
        def step(index, _):
            for lane in range(3):
                lanes = slice(lane * 128, lane * 128 + 128)
                low = ref[rows_at(base + (3 * side + index) * 8, 8), lanes]
                ref[rows_at(base + ((3 + half) * side + index) * 8, 8), lanes] = pltpu.roll(low, 4, 0) * top
                high = ref[rows_at(base + (half * side + index) * 8, 8), lanes]
                ref[rows_at(base + index * 8, 8), lanes] = pltpu.roll(high, 4, 0) * bottom
            return 0

        lax.fori_loop(0, 3 * side, step, 0)

    def all_halos(big, small):
        halos(big, 0, BIG_HALF, BIG_SIDE)
        for unit in range(UNITS):
            halos(small, unit * HALO_SMALL, SMALL_HALF, SMALL_SIDE)

    all_halos(halo_big, halo_small)

    kv_way = gather_core(kv_all, kv_way)
    arrived(kv_way)
    kv = jnp.transpose(flat(kv_all[...]).astype(F32))
    vec[...] = kv[64:80]
    for tap in range(TAPS):
        taps[tap] = jnp.broadcast_to(kv[tap : tap + 1] * (1.0 / KS), (8, C))

    def convolve(big, small, mirrored, finish, between):
        def tap_at(i, j, lanes):
            index = i * KS + j
            return taps[TAPS - 1 - index if mirrored else index, :, lanes]

        def row(step, _):
            h, lane = step // 3, lax.rem(step, 3)
            lanes = pl.ds(pl.multiple_of(lane * 128, 128), 128)
            sums = [None] * BIG_SIDE
            for i in range(KS):
                values = [big[rows_at(((h + i) * BIG_SIDE + w) * 8, 8), lanes] for w in range(BIG_SIDE)]
                for j in range(KS):
                    weight = tap_at(i, j, lanes)
                    for w in range(max(0, 3 - j), min(BIG_SIDE, BIG_SIDE + 3 - j)):
                        term = values[w + j - 3] * weight
                        sums[w] = term if sums[w] is None else sums[w] + term
            for w in range(BIG_SIDE):
                finish((h * BIG_SIDE + w) * 8, sums[w], lanes)
            return 0

        lax.fori_loop(0, BIG_HALF * 3, row, 0)
        between()

        def small_row(step, _):
            h, lane = step // 3, lax.rem(step, 3)
            lanes = pl.ds(pl.multiple_of(lane * 128, 128), 128)
            sums = [[None] * SMALL_SIDE for _ in range(UNITS)]
            for i in range(KS):
                values = [
                    [
                        small[rows_at(unit * HALO_SMALL + ((h + i) * SMALL_SIDE + w) * 8, 8), lanes]
                        for w in range(SMALL_SIDE)
                    ]
                    for unit in range(UNITS)
                ]
                for j in range(KS):
                    weight = tap_at(i, j, lanes)
                    for w in range(max(0, 3 - j), min(SMALL_SIDE, SMALL_SIDE + 3 - j)):
                        for unit in range(UNITS):
                            term = values[unit][w + j - 3] * weight
                            old = sums[unit][w]
                            sums[unit][w] = term if old is None else old + term
            for unit in range(UNITS):
                for w in range(SMALL_SIDE):
                    finish(BIG_ROWS + unit * SMALL_ROWS + (h * SMALL_SIDE + w) * 8, sums[unit][w], lanes)
            return 0

        lax.fori_loop(0, SMALL_HALF * 3, small_row, 0)

    def keep_conv(start, value, lanes):
        conv[rows_at(start, 8), lanes] = value

    ways = {}
    up_way = gather_plane(up_all, up_way)
    ways["down"] = down_way
    ways["strided"] = strided_way

    def weights_on():
        ways["down"] = gather_plane(down_all, ways["down"])
        ways["strided"] = gather_plane(strided_all, ways["strided"])
        ways["up"] = gather_core(up_all, up_way)

    convolve(halo_big, halo_small, False, keep_conv, weights_on)

    def for_tiles(run):
        def big_tile(index, _):
            run(index * 112, 112, big_factor, halo_big, dhalo_big, 336 + index * 112)
            return 0

        lax.fori_loop(0, BIG_HALF, big_tile, 0)

        def small_tile(index, _):
            run(BIG_ROWS + index * 144, 144, small_factor, halo_small, dhalo_small, index * HALO_SMALL + 144)
            return 0

        lax.fori_loop(0, UNITS, small_tile, 0)

    def fold(value):
        return jnp.sum(value.reshape(-1, 8, value.shape[-1]), axis=0)

    def mean_of(value):
        return jnp.sum(value, axis=-1, keepdims=True) * (1.0 / C)

    def wide(ref, rows):
        value = ref[rows, :]
        return jnp.concatenate([value, value, value], axis=1)

    def norm_one(start, size, *_):
        rows = rows_at(start, size)
        value = conv[rows, :] + vector_row(V_BIAS_DW)
        centered = value - mean_of(value)
        scale = lax.rsqrt(mean_of(centered * centered) + EPSILON)
        unit = centered * scale
        conv[rows, :] = unit
        rstd_one[rows, :] = jnp.broadcast_to(scale, (size, 128))
        normed[pl.ds(pl.multiple_of(start, 16), size), :] = (
            unit * vector_row(V_GAIN_ONE) + vector_row(V_OFFSET_ONE)
        ).astype(BF16)

    for_tiles(norm_one)

    def up_tile(index, _):
        rows = pl.ds(pl.multiple_of(index * TILE, 16), TILE)
        left = normed[rows, :]
        for chunk in range(FF // CHUNK):
            span = slice(chunk * CHUNK, (chunk + 1) * CHUNK)
            bias = vector_row(V_BIAS_UP + chunk)
            pre = (
                lax.dot_general(left, flat(up_all[chunk]), (((1,), (1,)), ((), ())), preferred_element_type=F32)
                * UP_SCALE
                + bias
            )
            whole = 0.5 + 0.5 * lax.erf(pre * math.sqrt(0.5))
            density = jnp.exp(pre * pre * -0.5) * (1.0 / math.sqrt(2.0 * math.pi))
            hidden[rows, span] = (pre * whole).astype(BF16)
            slope[rows, span] = whole + pre * density
        return 0

    arrived(ways["up"])
    lax.fori_loop(0, ROWS // TILE, up_tile, 0)
    ways["down"] = gather_core(down_all, ways["down"])
    arrived(ways["down"])

    def branch_tile(index, _):
        rows = pl.ds(pl.multiple_of(index * TILE, 16), TILE)
        branch[rows, :] = nn(hidden[rows, :], flat(down_all[...])) * DOWN_SCALE + vector_row(V_BIAS_DOWN)
        return 0

    lax.fori_loop(0, ROWS // TILE, branch_tile, 0)
    ways["strided"] = gather_core(strided_all, ways["strided"])

    def scaled(value, factor):
        return (value.reshape(-1, 8, C) * factor[None]).reshape(-1, C)

    def norm_two(start, size, factor, field, _, offset):
        rows = rows_at(start, size)
        value = field[rows_at(offset, size), :] + scaled(vector_row(V_SCALE) * branch[rows, :], factor)
        centered = value - mean_of(value)
        scale = lax.rsqrt(mean_of(centered * centered) + EPSILON)
        unit = centered * scale
        xhat[rows, :] = unit
        rstd_two[rows, :] = jnp.broadcast_to(scale, (size, 128))
        zeta[pl.ds(pl.multiple_of(start, 16), size), :] = (
            unit * vector_row(V_GAIN_TWO) + vector_row(V_OFFSET_TWO)
        ).astype(BF16)

    for_tiles(norm_two)

    def block_spans(base, count, hh, half_side):
        for half in range(2):
            h = half * half_side + hh
            p, a = h // 2, lax.rem(h, 2)
            for b in range(2):
                yield (
                    pl.ds(pl.multiple_of(base + p * count, 16), count),
                    pl.ds(pl.multiple_of((2 * a + b) * C, 128), C),
                )

    def block_rows(source, matrix, base, count, hh, half_side):
        picked = nn(matrix, source).astype(BF16)
        for index, span in enumerate(block_spans(base, count, hh, half_side)):
            blocks[span] = picked[index * count : (index + 1) * count]

    def big_blocks(hh, _):
        block_rows(zeta[pl.ds(pl.multiple_of(hh * 112, 16), 112), :], block_big, 0, 32, hh, 7)
        return 0

    lax.fori_loop(0, BIG_HALF, big_blocks, 0)
    for unit in range(UNITS):
        def small_blocks(hh, _):
            source = zeta[pl.ds(pl.multiple_of(BIG_ROWS + unit * SMALL_ROWS + hh * 48, 16), 48), :]
            block_rows(source, block_small, BLOCK_BIG + unit * 48, 16, hh, 3)
            return 0

        lax.fori_loop(0, SMALL_HALF, small_blocks, 0)

    g_rows[...] = g_wide[...].astype(BF16)
    bias_out_grad = jnp.sum(g_wide[...], axis=0, keepdims=True)
    d_vec[V_BIAS_OUT, 0:1, :] = bias_out_grad[:, :C]
    d_vec[V_BIAS_OUT + 1, 0:1, :] = bias_out_grad[:, C:]

    def strided_grad(index, _):
        span = pl.ds(pl.multiple_of(index * C, 128), C)
        d_strided[index] = (
            (
                lax.dot_general(blocks[:, span], g_rows[...], (((0,), (0,)), ((), ())), preferred_element_type=F32)
                * STRIDED_SCALE
            )
            .astype(BF16)
            .reshape(2, 192, C2)
        )
        return 0

    lax.fori_loop(0, 4, strided_grad, 0)
    ways["d_strided"] = reduce_core(d_strided, strided_core)
    arrived(ways["strided"])

    bias_out = jnp.concatenate([vector_row(V_BIAS_OUT), vector_row(V_BIAS_OUT + 1)], axis=1)

    for chunk in range(3):
        span = slice(chunk * 256, chunk * 256 + 256)
        g_wide[:, span] = nn(blocks[...], flat(strided_all[:, :, :, span])) * STRIDED_SCALE + bias_out[:, span]
    for micro in range(2):
        for p in range(7):
            start = p * 32 + micro * 16
            out_big_ref[micro, p] = g_wide[start : start + 14, :].reshape(7, 2, C2)
    for unit in range(UNITS):
        for p in range(3):
            for crop in range(2):
                start = BLOCK_BIG + (unit * 3 + p) * 16 + crop * 8
                out_small_ref[2 * unit + crop, p] = g_wide[start : start + 6, :].reshape(3, 2, C2)

    def block_grad(index, _):
        span = pl.ds(pl.multiple_of(index * 384, 128), 384)
        blocks[:, span] = (
            lax.dot_general(
                g_rows[...], flat(strided_all[index]), (((1,), (1,)), ((), ())), preferred_element_type=F32
            )
            * STRIDED_SCALE
        ).astype(BF16)
        return 0

    lax.fori_loop(0, 4, block_grad, 0)

    def unblock(matrix, base, count, hh, half_side):
        parts = jnp.concatenate([blocks[span] for span in block_spans(base, count, hh, half_side)], axis=0)
        return lax.dot_general(matrix, parts, (((0,), (0,)), ((), ())), preferred_element_type=F32)

    def big_unblock(hh, _):
        d_zeta[rows_at(hh * 112, 112), :] = unblock(block_big, 0, 32, hh, 7)
        return 0

    lax.fori_loop(0, BIG_HALF, big_unblock, 0)
    for unit in range(UNITS):
        def small_unblock(hh, _):
            d_zeta[rows_at(BIG_ROWS + unit * SMALL_ROWS + hh * 48, 48), :] = unblock(
                block_small, BLOCK_BIG + unit * 48, 16, hh, 3
            )
            return 0

        lax.fori_loop(0, SMALL_HALF, small_unblock, 0)

    ways["d_strided"] = reduce_plane(d_strided, strided_core, strided_plane, ways["d_strided"])

    for index in range(11):
        d_vec[index] = jnp.zeros((8, C), F32)

    def norm_two_back(start, size, factor, *_):
        rows = rows_at(start, size)
        unit = xhat[rows, :]
        grad = d_zeta[rows, :]
        d_vec[V_GAIN_TWO] += fold(grad * unit)
        d_vec[V_OFFSET_TWO] += fold(grad)
        inner = grad * vector_row(V_GAIN_TWO)
        mixed = (inner - mean_of(inner) - unit * mean_of(inner * unit)) * wide(rstd_two, rows)
        d_mixed[rows, :] = mixed
        kept = scaled(mixed, factor)
        d_vec[V_SCALE] += fold(kept * branch[rows, :])
        lowered = (kept * vector_row(V_SCALE)).astype(BF16)
        d_branch[pl.ds(pl.multiple_of(start, 16), size), :] = lowered
        d_vec[V_BIAS_DOWN] += fold(lowered.astype(F32))

    for_tiles(norm_two_back)

    d_bias_up[...] = jnp.zeros_like(d_bias_up)

    def down_tile(index, _):
        rows = pl.ds(pl.multiple_of(index * TILE, 16), TILE)
        left = d_branch[rows, :]
        for chunk in range(FF // CHUNK):
            span = slice(chunk * CHUNK, (chunk + 1) * CHUNK)
            d_hidden = (
                lax.dot_general(left, flat(down_all[chunk]), (((1,), (1,)), ((), ())), preferred_element_type=F32)
                * DOWN_SCALE
            )
            lowered = (d_hidden * slope[rows, span]).astype(BF16)
            d_pre[rows, span] = lowered
            d_bias_up[:, span] += fold(lowered.astype(F32))
        d_normed[rows, :] = (nn(d_pre[rows, :], flat(up_all[...])) * UP_SCALE).astype(BF16)
        return 0

    lax.fori_loop(0, ROWS // TILE, down_tile, 0)

    def outer(left, right, scale):
        product = lax.dot_general(left, right, (((0,), (0,)), ((), ())), preferred_element_type=F32)
        return (product * scale).astype(BF16).reshape(2, 192, C)

    def down_grad(index, _):
        span = pl.ds(pl.multiple_of(index * C, 128), C)
        d_down[index] = outer(hidden[:, span], d_branch[...], DOWN_SCALE)
        return 0

    def up_grad(index, _):
        span = pl.ds(pl.multiple_of(index * C, 128), C)
        d_up[index] = outer(d_pre[:, span], normed[...], UP_SCALE)
        return 0

    lax.fori_loop(0, 4, down_grad, 0)
    ways["d_down"] = reduce_core(d_down, down_core)
    lax.fori_loop(0, 4, up_grad, 0)
    ways["d_up"] = reduce_core(d_up, up_core)
    ways["d_down"] = reduce_plane(d_down, down_core, down_plane, ways["d_down"])

    def norm_one_back(start, size, _, __, target, offset):
        rows = rows_at(start, size)
        unit = conv[rows, :]
        grad = d_normed[pl.ds(pl.multiple_of(start, 16), size), :].astype(F32)
        d_vec[V_GAIN_ONE] += fold(grad * unit)
        d_vec[V_OFFSET_ONE] += fold(grad)
        inner = grad * vector_row(V_GAIN_ONE)
        result = (inner - mean_of(inner) - unit * mean_of(inner * unit)) * wide(rstd_one, rows)
        d_vec[V_BIAS_DW] += fold(result)
        target[rows_at(offset, size), :] = result

    for_tiles(norm_one_back)
    ways["d_up"] = reduce_plane(d_up, up_core, up_plane, ways["d_up"])
    ways["d_strided"] = reduce_line(strided_core, strided_plane, strided_line, ways["d_strided"])
    all_halos(dhalo_big, dhalo_small)

    def tap_grads(step, _):
        i, lane = step // 3, lax.rem(step, 3)
        lanes = pl.ds(pl.multiple_of(lane * 128, 128), 128)

        def image_row(side, field, grad, field_base, grad_base, sums):
            inputs = [field[rows_at(field_base + w * 8, 8), lanes] for w in range(side)]
            outer = [grad[rows_at(grad_base + w * 8, 8), lanes] for w in range(side)]
            result = []
            for j in range(KS):
                total = sums[j]
                for w in range(max(0, 3 - j), min(side, side + 3 - j)):
                    total = total + inputs[w + j - 3] * outer[w]
                result.append(total)
            return tuple(result)

        sums = tuple(jnp.zeros((8, 128), F32) for _ in range(KS))
        sums = lax.fori_loop(
            0,
            BIG_HALF,
            lambda h, carry: image_row(
                BIG_SIDE, halo_big, dhalo_big, (h + i) * 112, (h + 3) * 112, carry
            ),
            sums,
        )
        for unit in range(UNITS):
            sums = lax.fori_loop(
                0,
                SMALL_HALF,
                lambda h, carry, base=unit * HALO_SMALL: image_row(
                    SMALL_SIDE, halo_small, dhalo_small, base + (h + i) * 48, base + (h + 3) * 48, carry
                ),
                sums,
            )
        for j in range(KS):
            d_taps[i * KS + j, :, lanes] = sums[j]
        return 0

    lax.fori_loop(0, KS * 3, tap_grads, 0)

    d_kv[56:64, :] = jnp.zeros((8, C), F32)
    for tap in range(TAPS):
        d_kv[tap : tap + 1, :] = jnp.sum(d_taps[tap], axis=0, keepdims=True) * (1.0 / KS)
    for index in range(11):
        if V_BIAS_UP <= index < V_BIAS_UP + UP_ROWS:
            continue
        d_kv[TAPS + index : TAPS + index + 1, :] = jnp.sum(d_vec[index], axis=0, keepdims=True)
    d_kv[TAPS + V_BIAS_OUT : TAPS + V_BIAS_OUT + 1, :] = d_vec[V_BIAS_OUT, 0:1, :]
    d_kv[TAPS + V_BIAS_OUT + 1 : TAPS + V_BIAS_OUT + 2, :] = d_vec[V_BIAS_OUT + 1, 0:1, :]
    bias_up_grad = jnp.sum(d_bias_up[...], axis=0, keepdims=True)
    for index in range(UP_ROWS):
        d_kv[TAPS + V_BIAS_UP + index : TAPS + V_BIAS_UP + index + 1, :] = bias_up_grad[
            :, index * C : (index + 1) * C
        ]

    ways["d_kv"] = [send(d_kv, kv_core, twin)]

    def kv_rows(index):
        return pl.ds(pl.multiple_of(index * 16, 16), 16)

    def kv_reduce_plane(copies):
        arrived(copies)
        kv_core[...] += d_kv[...]
        return [send(kv_core.at[kv_rows(flanks[index])], kv_plane.at[index], on_plane(index)) for index in range(3)]

    def kv_reduce_line(copies):
        arrived(copies)
        kv_line[0] = kv_core[kv_rows(rank), :] + kv_plane[0] + kv_plane[1] + kv_plane[2]
        return [send(kv_line.at[0], kv_line.at[offset], on_line(offset)) for offset in (1, 2, 3)]

    def kv_reduce_back(copies):
        arrived(copies)
        total = jnp.zeros((16, C), F32)
        for index in range(PLANES):
            total = total + kv_line[lax.rem(line - index + PLANES, PLANES)]
        kv_sum[kv_rows(rank), :] = total
        part = kv_sum.at[kv_rows(rank)]
        return [send(part, part, on_plane(index)) for index in range(3)]

    def add_grad(start, value, lanes):
        d_mixed[rows_at(start, 8), lanes] += value

    def gradients_on():
        ways["d_kv"] = kv_reduce_plane(ways["d_kv"])
        ways["d_down"] = reduce_line(down_core, down_plane, down_line, ways["d_down"])
        ways["d_strided"] = reduce_back(strided_line, strided_sum, ways["d_strided"])

    convolve(dhalo_big, dhalo_small, True, add_grad, gradients_on)
    ways["d_kv"] = kv_reduce_line(ways["d_kv"])
    ways["d_up"] = reduce_line(up_core, up_plane, up_line, ways["d_up"])
    ways["d_down"] = reduce_back(down_line, down_sum, ways["d_down"])

    def restore(matrix, value):
        high = value.astype(BF16)
        low = (value - high.astype(F32)).astype(BF16)
        return nn(matrix, high) + nn(matrix, low)

    def grad_rows(hh, _):
        natural = restore(gather_big, d_mixed[rows_at(hh * 112, 112), :])
        for half in range(2):
            for micro in range(2):
                start = (half * 2 + micro) * 32
                grad_big_ref[micro, half * 7 + hh] = natural[start : start + 28].reshape(14, 2, C)
        return 0

    lax.fori_loop(0, BIG_HALF, grad_rows, 0)
    for unit in range(UNITS):
        def small_grad_rows(hh, _):
            natural = restore(gather_small, d_mixed[rows_at(BIG_ROWS + unit * SMALL_ROWS + hh * 48, 48), :])
            for half in range(2):
                for crop in range(2):
                    start = (half * 2 + crop) * 16
                    grad_small_ref[2 * unit + crop, half * 3 + hh] = natural[start : start + 12].reshape(6, 2, C)
            return 0

        lax.fori_loop(0, SMALL_HALF, small_grad_rows, 0)

    ways["d_kv"] = kv_reduce_back(ways["d_kv"])
    ways["d_up"] = reduce_back(up_line, up_sum, ways["d_up"])
    for name, final, target in (
        ("d_strided", strided_sum, strided_out),
        ("d_down", down_sum, down_out),
        ("d_up", up_sum, up_out),
    ):
        arrived(ways[name])
        target[...] = final[...]
    arrived(ways["d_kv"])
    kv_turn[...] = jnp.transpose(kv_sum[...])
    kv_out[...] = kv_turn[pl.ds(pl.multiple_of(dp_rank * PIECE, 16), PIECE), :]
    for copy in pending:
        copy.wait_send()


def fused_step(big_crops, small_crops, big_cot, small_cot, keep, kernel_t, vector, up_t, down, strided):
    any_spec = pl.BlockSpec(memory_space=pl.ANY)
    vmem = pl.BlockSpec(memory_space=pltpu.VMEM)
    shape = jax.ShapeDtypeStruct
    big_order, small_order = (0, 2, 3, 1, 4), (1, 2, 3, 0, 4)
    results = pl.pallas_call(
        step_kernel,
        out_shape=(
            shape((2, 7, 7, 2, C2), F32),
            shape((6, 3, 3, 2, C2), F32),
            shape((2, 14, 14, 2, C), F32),
            shape((6, 6, 6, 2, C), F32),
            shape((PIECE, 64), F32),
            shape((192, C), BF16),
            shape((192, C), BF16),
            shape((192, C2), BF16),
        ),
        in_specs=[any_spec] * 4 + [pl.BlockSpec(memory_space=pltpu.SMEM)] + [vmem] * 5,
        out_specs=[vmem] * 8,
        scratch_shapes=[
            pltpu.VMEM((2, 14, 14, 2, C), BF16),
            pltpu.VMEM((6, 6, 6, 8, C), BF16),
            pltpu.VMEM((2, 7, 7, 2, C2), BF16),
            pltpu.VMEM((6, 3, 3, 8, C2), BF16),
            pltpu.VMEM((HALO_BIG, C), F32),
            pltpu.VMEM((UNITS * HALO_SMALL, C), F32),
            pltpu.VMEM((TAPS, 8, C), F32),
            pltpu.VMEM((16, C), F32),
            pltpu.VMEM((ROWS, C), F32),
            pltpu.VMEM((ROWS, 128), F32),
            pltpu.VMEM((ROWS, C), BF16),
            pltpu.VMEM((ROWS, FF), BF16),
            pltpu.VMEM((ROWS, FF), F32),
            pltpu.VMEM((ROWS, C), F32),
            pltpu.VMEM((ROWS, C), F32),
            pltpu.VMEM((ROWS, 128), F32),
            pltpu.VMEM((ROWS, C), BF16),
            pltpu.VMEM((BLOCKS, 4 * C), BF16),
            pltpu.VMEM((BLOCKS, C2), F32),
            pltpu.VMEM((BLOCKS, C2), BF16),
            pltpu.VMEM((ROWS, C), F32),
            pltpu.VMEM((ROWS, C), F32),
            pltpu.VMEM((ROWS, C), BF16),
            pltpu.VMEM((ROWS, FF), BF16),
            pltpu.VMEM((ROWS, C), BF16),
            pltpu.VMEM((HALO_BIG, C), F32),
            pltpu.VMEM((UNITS * HALO_SMALL, C), F32),
            pltpu.VMEM((TAPS, 8, C), F32),
            pltpu.VMEM((13, 8, C), F32),
            pltpu.VMEM((8, FF), F32),
            pltpu.VMEM((4, 2, 48, 128), BF16),
            pltpu.VMEM((4, 2, 192, C), BF16),
            pltpu.VMEM((4, 2, 192, C), BF16),
            pltpu.VMEM((4, 2, 192, C2), BF16),
            pltpu.VMEM((4, 2, 192, C), BF16),
            pltpu.VMEM((4, 2, 192, C), BF16),
            pltpu.VMEM((4, 2, 192, C2), BF16),
            pltpu.VMEM((4, 192, C), BF16),
            pltpu.VMEM((4, 192, C), BF16),
            pltpu.VMEM((4, 192, C2), BF16),
            pltpu.VMEM((3, 4, PIECE, C), BF16),
            pltpu.VMEM((3, 4, PIECE, C), BF16),
            pltpu.VMEM((3, 4, PIECE, C2), BF16),
            pltpu.VMEM((7, PIECE, C), BF16),
            pltpu.VMEM((7, PIECE, C), BF16),
            pltpu.VMEM((7, PIECE, C2), BF16),
            pltpu.VMEM((192, C), BF16),
            pltpu.VMEM((192, C), BF16),
            pltpu.VMEM((192, C2), BF16),
            pltpu.VMEM((64, C), F32),
            pltpu.VMEM((64, C), F32),
            pltpu.VMEM((3, 16, C), F32),
            pltpu.VMEM((4, 16, C), F32),
            pltpu.VMEM((64, C), F32),
            pltpu.VMEM((C, 64), F32),
            pltpu.SemaphoreType.DMA((4,)),
            pltpu.SemaphoreType.DMA((83,)),
            pltpu.SemaphoreType.DMA((83,)),
        ],
        compiler_params=pltpu.CompilerParams(vmem_limit_bytes=(63 << 20) + (1 << 19), collective_id=0, has_side_effects=True),
    )(
        big_crops.transpose(big_order),
        small_crops.transpose(small_order),
        big_cot.transpose(big_order),
        small_cot.transpose(small_order),
        keep,
        kernel_t,
        vector,
        up_t,
        down,
        strided,
    )
    back_big, back_small = (0, 3, 1, 2, 4), (3, 0, 1, 2, 4)
    return (
        results[0].transpose(back_big),
        results[1].transpose(back_small),
        results[2].transpose(back_big),
        results[3].transpose(back_small),
        *results[4:],
    )


def body(big_crops, small_crops, big_cot, small_cot, drop_mask, *state):
    sections, rank = lax.axis_size("section"), lax.axis_index("section")
    micro_count = big_crops.shape[0]
    fits = (
        micro_count == 2 * sections
        and big_crops.shape[1:] == (BIG_IMG, BIG_SIDE, BIG_SIDE, C)
        and small_crops.shape[1:] == (SMALL_IMG, SMALL_SIDE, SMALL_SIDE, C)
        and drop_mask.shape[1] == 1
        and (sections, lax.axis_size("dp")) == (4, 8)
    )
    if not fits:
        return plain_body(big_crops, small_crops, big_cot, small_cot, drop_mask, *state)
    masters, moments, averages = state[0::3], state[1::3], state[2::3]
    turned = (True, False, True, False, False)
    masters, moments, averages = (
        [jnp.transpose(array) if turn else array for array, turn in zip(group, turned)]
        for group in (masters, moments, averages)
    )
    keep = lax.dynamic_slice_in_dim(drop_mask, rank * 2, 2, 0)
    out_big, out_small, grad_big, grad_small, d_kv, d_up, d_down, d_strided = fused_step(
        big_crops, small_crops, big_cot, small_cot, keep, *masters
    )
    gradients = (
        d_kv[:, :TAPS],
        jnp.transpose(d_kv[:, TAPS : TAPS + masters[1].shape[0]]),
        d_up.astype(F32),
        d_down.astype(F32),
        d_strided.astype(F32),
    )
    pixel_total = (
        lax.axis_size("dp")
        * micro_count
        * (math.prod(big_crops.shape[1:4]) + math.prod(small_crops.shape[1:4]))
    )
    updates = []
    for position in range(5):
        step_rate = RATES[position] * math.sqrt(FANS[position] / pixel_total)
        moment_next = MOMENTUM * moments[position] + gradients[position]
        weight_next = masters[position] - step_rate * (gradients[position] + MOMENTUM * moment_next)
        average_next = AVERAGING * averages[position] + (1.0 - AVERAGING) * weight_next
        new = (weight_next, moment_next, average_next)
        updates += [jnp.transpose(array) if turned[position] else array for array in new]
    return (out_big, out_small, grad_big, grad_small, *updates)


def solution(mesh):
    crops = P(None, "dp", None, None, None)
    owned = P("section", "dp", None, None, None)
    weights = (P(None, "dp"),) * 9 + (P("dp", None),) * 6
    return jax.shard_map(
        body,
        mesh=mesh,
        in_specs=(crops,) * 4 + (P(None, "dp"),) + weights,
        out_specs=(owned,) * 4 + weights,
        check_vma=False,
    )
```

time: 2800 us -> 118 us (0.04); the launches traced: 2760 us -> 117 us
  waiting for transfers between devices: 890 us -> 0 us
  local copies, waits for them, and re-layouts: 591 us -> 9.69 us
  starting transfers between devices: 380 us -> 0 us
  matrix products: 290 us -> 0 us
  other arithmetic: 277 us -> 6.36 us
  loops' own time: 218 us -> 0 us
  blocking collectives: 103 us -> 0 us
  Pallas kernels: 0 us -> 101 us
    ppermute x88 -> x0, waiting for transfers between devices: 593 us -> none  [shifted(): return lax.ppermute(shard, axis, pairs)]
    ppermute x88 -> x0, starting transfers between devices: 380 us -> none  [shifted(): return lax.ppermute(shard, axis, pairs)]
    conv_general_dilated x64 -> x0, matrix products: 290 us -> none  [depthwise(): lax.conv_general_dilated(crop_field, kernel.reshape(KS, KS, 1, channels),...]
    another operation x24 -> x0, loops' own time: 218 us -> none  [the longest x11 168 us: behind(): lax.switch(jnp.where(is_active, section_rank, sections), backward_list +...]
    psum x1 -> x0, waiting for transfers between devices: 147 us -> none  [body(): lax.psum((totals[0], totals[1], totals[2], totals[3], totals[4]), ('secti...]
    another operation x60 -> x0, local copies, waits for them, and re-layouts: 139 us -> none
    dynamic_slice x110 -> x1, local copies, waits for them, and re-layouts: 118 us -> 0.07 us  [body(): keep = lax.dynamic_slice_in_dim(drop_mask, rank * 2, 2, 0)]
    reduce_scatter x3 -> x0, waiting for transfers between devices: 107 us -> none  [the longest x1 64.4 us: body(): lax.psum_scatter(grad_terms[0], 'section', scatter_dimension=0, tiled=True)]
  transfers between devices with their start and end apart: 96 -> 0, of which waited for: 38 -> 0; matrix products, arithmetic and copies ran while one was open for 31% -> 0% of each run, Pallas kernels for 0% -> 0%
where the time goes in v1:
time: 118 us; the launch traced here: 117 us
  Pallas kernels  101 us (86%)
  local copies, waits for them, and re-layouts  9.69 us (8%)
  other arithmetic  6.36 us (5%)
    pallas_call x1, Pallas kernels, fused_step(): pl.pallas_call(step_kernel, out_shape=(shape((2, 7, 7, 2, C2), F32), shap...  101 us
    unnamed x37, local copies, waits for them, and re-layouts  9.62 us
    transpose x2, other arithmetic, body(): jnp.transpose(array)  4.2 us

profile of v1, /device:TPU:0, one launch (start us, length us, event | category | flops | bytes accessed | tf_op | source)
XLA Modules:
  0.0 117.4 jit_solution(4661848832359917225)
XLA Ops:
  0.7 0.0 copy-start
  0.7 0.6 copy-done
  1.3 0.1 constant_dynamic-slice_fusion
  1.4 0.7 copy.56.keep_ref
  2.0 0.8 copy.47
  2.8 0.8 copy.51
  3.6 0.8 copy.50
  4.4 0.0 copy-start.10
  4.4 0.0 copy-start.11
  4.4 0.0 copy-start.12
  4.4 0.0 copy-start.3
  4.4 100.6 %shard_map.339 = (f32[2,7,7,2,768]{4,3,2,1,0:T(2,128)}, f32[6,3,3,2,768]{4,3,2,1,0:T(2,128)}, f32[2,14,14,2,384]{4,3,2,1,0:T(2,128)}, f32[6,6,6,2,384]{4,3,2,1,0...) custom-call(bf16[8,14,14,2,384]{4,3,2,1,0:T(2,128)(2,1)} %bitcast.73, ...), custom_call_target="tpu_custom_call" | custom-call | tf_op jit(solution)/shard_map/pallas_call | solution.py:910
  105.0 0.8 add_multiply_fusion.2
  105.8 0.7 copy.55
  106.5 0.7 copy.53
  107.1 0.7 copy.54
  107.8 0.0 copy-done.10
  107.8 0.0 copy-done.11
  107.8 0.0 copy-done.12
  107.8 1.4 %fusion.12 = (f32[49,48]{0,1:T(8,128)}, f32[49,48]{0,1:T(8,128)}, f32[49,48]{0,1:T(8,128)}) fusion(f32[49,48]{0,1:T(8,128)S(1)} %copy-done.11, f32[49,48]{0,1:T(8,128)S(1)} %copy-done.12, f32[48,64]{1,0:T(8,128)} %get-tuple-element.31, f32[49,48]{0,1:T(8,128)S(1)} %copy-done.10), kind=kLoop, calls=%fused_computation.24 | loop fusion | flops 18816 | bytes 65856 | tf_op jit(solution)/shard_map/transpose | solution.py:1048
  109.2 0.0 copy-done.3
  109.2 0.0 copy-start.1
  109.2 0.0 copy-start.6
  109.2 0.0 copy-start.7
  109.2 0.0 copy-start.9
  109.2 2.8 %fusion.7 = (f32[384,192]{0,1:T(8,128)}, f32[384,192]{0,1:T(8,128)}, f32[384,192]{0,1:T(8,128)}, f32[192,384]{1,0:T(8,128)}, f32[192,384]{1,0:T(8,128)}, /*index=5*/f32[192,384]{1,0:T(8,128)}) fusion(f32[384,192]{0,1:T(8,128)} %param.33, f32[384,192]{0,1:T(8,128)} %param.32, bf16[192,384]{1,0:T(8,128)(2,1)} %get-tuple-element.32, ...), kind=kLoop, calls=%fused_computation.15 | loop fusion | flops 1327104 | bytes 3833856 | tf_op jit(solution)/shard_map/transpose | solution.py:1048
  112.1 0.0 copy-done.1
  112.1 0.0 copy-done.6
  112.1 0.0 copy-done.7
  112.1 0.0 copy-done.9
  112.1 0.0 copy-start.5
  112.1 0.0 copy-start.8
  112.1 1.3 %add_multiply_fusion = (f32[192,768]{1,0:T(8,128)}, f32[192,768]{1,0:T(8,128)}, f32[192,768]{1,0:T(8,128)}) fusion(f32[192,768]{1,0:T(8,128)S(1)} %copy-done.6, f32[192,768]{1,0:T(8,128)S(1)} %copy-done.1, bf16[192,768]{1,0:T(8,128)(2,1)S(1)} %copy-done.9, f32[192,768]{1,0:T(8,128)S(1)} %copy-done.7), kind=kLoop, calls=%fused_computation.4 | loop fusion | flops 1327104 | bytes 3833856 | tf_op jit(solution)/shard_map/add | solution.py:1046
  113.5 0.0 copy-start.2
  113.5 0.0 copy-done.5
  113.5 0.8 copy.61
  114.3 0.0 copy-done.8
  114.3 0.7 copy.62
  115.0 0.0 copy-done.2
  115.0 0.0 copy-start.4
  115.0 1.0 copy.63
  116.0 0.5 copy-done.4
  116.5 0.8 copy.64
Async XLA Ops:
  0.7 0.7 copy-start
  4.4 103.4 %copy-start.10 = (f32[49,48]{0,1:T(8,128)S(1)}, f32[49,48]{0,1:T(8,128)}, u32[]{:S(2)}) copy-start(f32[49,48]{0,1:T(8,128)} %param.25) | copy-start | bytes 28228
  4.4 103.4 %copy-start.11 = (f32[49,48]{0,1:T(8,128)S(1)}, f32[49,48]{0,1:T(8,128)}, u32[]{:S(2)}) copy-start(f32[49,48]{0,1:T(8,128)} %param.27) | copy-start | bytes 28228
  4.4 103.4 %copy-start.12 = (f32[49,48]{0,1:T(8,128)S(1)}, f32[49,48]{0,1:T(8,128)}, u32[]{:S(2)}) copy-start(f32[49,48]{0,1:T(8,128)} %param.26) | copy-start | bytes 28228
  4.4 104.8 %copy-start.3 = (f32[384,192]{0,1:T(8,128)S(1)}, f32[384,192]{0,1:T(8,128)}, u32[]{:S(2)}) copy-start(f32[384,192]{0,1:T(8,128)} %param.31) | copy-start | bytes 884740
  109.2 2.9 %copy-start.1 = (f32[192,768]{1,0:T(8,128)S(1)}, f32[192,768]{1,0:T(8,128)}, u32[]{:S(2)}) copy-start(f32[192,768]{1,0:T(8,128)} %strided_shard.1) | copy-start | bytes 1769476
  109.2 2.9 %copy-start.6 = (f32[192,768]{1,0:T(8,128)S(1)}, f32[192,768]{1,0:T(8,128)}, u32[]{:S(2)}) copy-start(f32[192,768]{1,0:T(8,128)} %param.39) | copy-start | bytes 1769476
  109.2 2.9 %copy-start.7 = (f32[192,768]{1,0:T(8,128)S(1)}, f32[192,768]{1,0:T(8,128)}, u32[]{:S(2)}) copy-start(f32[192,768]{1,0:T(8,128)} %param.38) | copy-start | bytes 1769476
  109.2 2.9 %copy-start.9 = (bf16[192,768]{1,0:T(8,128)(2,1)S(1)}, bf16[192,768]{1,0:T(8,128)(2,1)}, u32[]{:S(2)}) copy-start(bf16[192,768]{1,0:T(8,128)(2,1)} %get-tuple-element.34) | copy-start | bytes 884740
  112.1 1.4 %copy-start.5 = (f32[2,7,7,2,768]{4,3,2,1,0:T(2,128)S(1)}, f32[2,7,7,2,768]{4,3,2,1,0:T(2,128)}, u32[]{:S(2)}) copy-start(f32[2,7,7,2,768]{4,3,2,1,0:T(2,128)} %get-tuple-element.27) | copy-start | bytes 1806340
  112.1 2.2 %copy-start.8 = (f32[6,3,3,2,768]{4,3,2,1,0:T(2,128)S(1)}, f32[6,3,3,2,768]{4,3,2,1,0:T(2,128)}, u32[]{:S(2)}) copy-start(f32[6,3,3,2,768]{4,3,2,1,0:T(2,128)} %get-tuple-element.28) | copy-start | bytes 995332
  113.5 1.6 %copy-start.2 = (f32[2,14,14,2,384]{4,3,2,1,0:T(2,128)S(1)}, f32[2,14,14,2,384]{4,3,2,1,0:T(2,128)}, u32[]{:S(2)}) copy-start(f32[2,14,14,2,384]{4,3,2,1,0:T(2,128)} %get-tuple-element.29) | copy-start | bytes 3612676
  115.0 1.5 %copy-start.4 = (f32[6,6,6,2,384]{4,3,2,1,0:T(2,128)S(1)}, f32[6,6,6,2,384]{4,3,2,1,0:T(2,128)}, u32[]{:S(2)}) copy-start(f32[6,6,6,2,384]{4,3,2,1,0:T(2,128)} %get-tuple-element.30) | copy-start | bytes 1990660

commit v2 on v1

--- a/solution.py
+++ b/solution.py
@@ -1,3 +1,4 @@
+import functools
 import math
 
 import jax
@@ -199,6 +200,7 @@
 CHUNK = C
 PIECE = 48
 PLANES = 4
+COPIES = 118
 UP_SCALE, DOWN_SCALE, STRIDED_SCALE = 1 / math.sqrt(C), 1 / math.sqrt(FF), 1 / math.sqrt(4 * C)
 TAPS = KS * KS
 V_BIAS_DW, V_GAIN_ONE, V_OFFSET_ONE, V_BIAS_UP = 0, 1, 2, 3
@@ -210,7 +212,16 @@
 
 
 def rows_at(start, size):
-    return pl.ds(pl.multiple_of(start, 8), size)
+    return pl.ds(aligned(start, 8), size)
+
+
+def aligned(value, factor):
+    return value if isinstance(value, int) else pl.multiple_of(value, factor)
+
+
+def unrolled(count, step):
+    for index in range(count):
+        step(index, 0)
 
 
 def one_hot(shape, target, valid=None):
@@ -230,17 +241,17 @@
     big_hbm, small_hbm, big_cot_hbm, small_cot_hbm, keep_ref, kernel_ref, vector_ref, up_shard, down_shard, strided_shard,
     out_big_ref, out_small_ref, grad_big_ref, grad_small_ref, kv_out, up_out, down_out, strided_out,
     xb_raw, xs_raw, gb_raw, gs_raw, halo_big, halo_small, taps, vec, conv, rstd_one, normed,
-    hidden, slope, branch, xhat, rstd_two, zeta, blocks, g_wide, g_rows, d_zeta, d_mixed, d_branch, d_pre, d_normed,
+    hidden, slope, branch, xhat, rstd_two, zeta, blocks, d_blocks, g_wide, g_rows, d_branch, d_pre,
     dhalo_big, dhalo_small, d_taps, d_vec, d_bias_up,
-    kv_all, up_all, down_all, strided_all, d_up, d_down, d_strided,
-    up_core, down_core, strided_core, up_plane, down_plane, strided_plane, up_line, down_line, strided_line,
-    up_sum, down_sum, strided_sum, d_kv, kv_core, kv_plane, kv_line, kv_sum, kv_turn,
+    kv_all, w_all, d_all, landing, plane_in, totals, line_in, final,
+    d_kv, kv_part, kv_in, kv_sum,
     sems, send_sems, recv_sems,
 ):
-    pad_big = branch.at[0:896]
+    pad_big, d_zeta, d_normed, d_mixed = branch.at[0:896], dhalo_big.at[0:ROWS], zeta, xhat
     rank, dp_rank = lax.axis_index("section"), lax.axis_index("dp")
+    row, column = rank // 2, lax.rem(rank, 2)
     line, core = dp_rank // 2, lax.rem(dp_rank, 2)
-    flanks = (rank + 1 - 2 * lax.rem(rank, 2), rank + 2 - 4 * (rank // 2), 3 - rank)
+    flanks = (rank + 1 - 2 * column, rank + 2 - 4 * row, 3 - rank)
     twin = {"section": rank, "dp": dp_rank + 1 - 2 * core}
 
     def ahead(offset):
@@ -253,82 +264,124 @@
         return {"section": flanks[index], "dp": dp_rank}
 
     barrier = pltpu.get_barrier_semaphore()
-    for target in [twin] + [on_plane(index) for index in range(3)] + [on_line(offset) for offset in (1, 2, 3)]:
+    def on_group(offset):
+        return {"section": rank, "dp": lax.rem(dp_rank + offset, 8)}
+
+    for target in [on_plane(index) for index in range(3)] + [on_group(offset) for offset in range(1, 8)]:
         pl.semaphore_signal(barrier, inc=1, device_id=target, device_id_type=MESH)
 
-    pending = []
-
-    def send(source, target_ref, target):
-        index = len(pending)
+    made = []
+
+    def plan(source, target_ref, target):
+        index = len(made)
         copy = pltpu.make_async_remote_copy(
             source, target_ref, send_sems.at[index], recv_sems.at[index], device_id=target, device_id_type=MESH
         )
-        copy.start()
-        pending.append(copy)
+        made.append(copy)
         return copy
+
+    def same(ref, target):
+        return plan(ref, ref, target)
+
+    def go(copies):
+        for copy in copies:
+            copy.start()
 
     def arrived(copies):
         for copy in copies:
             copy.wait_recv()
 
     def piece(index):
-        return pl.ds(pl.multiple_of(index * PIECE, 16), PIECE)
-
-    def gather_line(ref, whole=False):
-        part = ref.at[line, core] if whole else ref.at[line, core, piece(rank)]
-        return [send(part, part, on_line(offset)) for offset in (1, 2, 3)]
-
-    def gather_plane(ref, copies):
-        result = []
-        for offset, copy in zip((1, 2, 3), copies):
-            copy.wait_recv()
-            part = ref.at[ahead(PLANES - offset), core, piece(rank)]
-            result += [send(part, part, on_plane(index)) for index in range(3)]
-        return result
-
-    def gather_core(ref, copies):
-        arrived(copies)
-        part = ref.at[:, core]
-        return [send(part, part, twin)]
-
-    def reduce_core(partial, landing):
-        return [send(partial.at[:, 1 - core], landing, twin)]
-
-    def reduce_plane(partial, landing, plane, copies):
-        arrived(copies)
+        return pl.ds(aligned(index * PIECE, 16), PIECE)
+
+    offsets = (1, 2, 3)
+
+    kv_ways = [same(kv_all.at[line, core], on_line(offset)) for offset in offsets]
+    kv_twin = [same(kv_all.at[:, core], twin)]
+    along, across, twins = [], [], []
+    for weight in range(4):
+        def part(offset, quarter):
+            return w_all.at[weight, ahead(PLANES - offset), core, piece(quarter)]
+
+        along.append([same(w_all.at[weight, line, core, piece(rank)], on_line(offset)) for offset in offsets])
+        across.append([[same(part(offset, rank), on_plane(index)) for offset in offsets] for index in range(3)])
+        twins.append([same(w_all.at[weight, :, core, piece(quarter)], twin) for quarter in (rank,) + flanks])
+
+    def pass_line(weight):
+        arrived(along[weight])
+        for copies in across[weight]:
+            go(copies)
+        go(twins[weight][:1])
+
+    def pass_plane(weight):
+        for index, copies in enumerate(across[weight]):
+            arrived(copies)
+            go(twins[weight][1 + index : 2 + index])
+
+    def held(weight):
+        arrived(twins[weight])
+
+    red_core, red_plane, red_line, red_back = [], [], [], []
+    corners = ((row, 1 - column), (1 - row, column), (1 - row, 1 - column))
+    for weight in range(4):
+        red_core.append([plan(d_all.at[weight, :, 1 - core], landing.at[weight], twin)])
+        red_plane.append(
+            [
+                plan(landing.at[weight, :, at_row, at_column], plane_in.at[weight, index], on_plane(index))
+                for index, (at_row, at_column) in enumerate(corners)
+            ]
+        )
+        red_line.append(
+            [plan(totals.at[weight, ahead(offset)], line_in.at[weight, offset - 1], on_line(offset)) for offset in offsets]
+        )
+        red_back.append([same(final.at[weight, rank], on_plane(index)) for index in range(3)])
+
+    def sum_core(weight):
+        arrived(red_core[weight])
+
+        def step(index, _):
+            landing[weight, index] = (
+                landing[weight, index].astype(F32) + d_all[weight, index, core].astype(F32)
+            ).astype(BF16)
+            return 0
+
+        lax.fori_loop(0, PLANES, step, 0)
+        go(red_plane[weight])
+
+    def sum_plane(weight):
+        arrived(red_plane[weight])
         for index in range(PLANES):
-            landing[index] = (landing[index].astype(F32) + partial[index, core].astype(F32)).astype(BF16)
-        return [
-            send(landing.at[:, piece(flanks[index])], plane.at[index], on_plane(index)) for index in range(3)
-        ]
-
-    def reduce_line(landing, plane, ways, copies):
-        arrived(copies)
-        result = []
-        for offset in (1, 2, 3, 0):
-            index = ahead(offset)
-            total = landing[index, piece(rank)].astype(F32)
+            total = landing[weight, index, row, column].astype(F32)
             for source in range(3):
-                total = total + plane[source, index].astype(F32)
-            if offset:
-                ways[offset - 1] = total.astype(BF16)
-                result.append(send(ways.at[offset - 1], ways.at[2 + offset], on_line(offset)))
-            else:
-                ways[6] = total.astype(BF16)
-        return result
-
-    def reduce_back(ways, final, copies):
-        arrived(copies)
-        total = ways[6].astype(F32)
-        for offset in (1, 2, 3):
-            total = total + ways[2 + offset].astype(F32)
-        final[piece(rank), :] = total.astype(BF16)
-        part = final.at[piece(rank)]
-        return [send(part, part, on_plane(index)) for index in range(3)]
-
-    up_all[line, core] = up_shard[...].astype(BF16)
-    down_all[line, core] = down_shard[...].astype(BF16)
-    strided_all[line, core] = strided_shard[...].astype(BF16)
+                total = total + plane_in[weight, source, index].astype(F32)
+            totals[weight, index] = total.astype(BF16)
+        go(red_line[weight])
+
+    def sum_line(weight):
+        arrived(red_line[weight])
+        total = totals[weight, line].astype(F32)
+        for offset in offsets:
+            total = total + line_in[weight, offset - 1].astype(F32)
+        final[weight, rank] = total.astype(BF16)
+        go(red_back[weight])
+
+    kv_across = [
+        plan(kv_part.at[lax.rem(dp_rank + offset, 8)], kv_in.at[offset - 1], on_group(offset)) for offset in range(1, 8)
+    ]
+    kv_back = [same(kv_sum.at[rank], on_plane(index)) for index in range(3)]
+
+    def kv_sum_group():
+        arrived(kv_across)
+        total = kv_part[dp_rank].astype(F32)
+        for index in range(7):
+            total = total + kv_in[index].astype(F32)
+        kv_sum[rank] = total
+        go(kv_back)
+
+    w_all[0, line, core] = up_shard[...].astype(BF16)
+    w_all[1, line, core] = down_shard[...].astype(BF16)
+    w_all[2, line, core] = strided_shard[:, :C].astype(BF16)
+    w_all[3, line, core] = strided_shard[:, C:].astype(BF16)
     put_taps = one_hot((TAPS, 128), lambda r: r)
     put_vector = one_hot((13, 128), lambda r: r + 64)
     kv_all[line, core] = (
@@ -337,11 +390,21 @@
             vector_ref[...].astype(BF16), put_vector, (((0,), (0,)), ((), ())), preferred_element_type=F32
         )
     ).astype(BF16)
-    pl.semaphore_wait(barrier, 7)
-    kv_way = gather_line(kv_all, True)
-    up_way = gather_line(up_all)
-    down_way = gather_line(down_all)
-    strided_way = gather_line(strided_all)
+    pl.semaphore_wait(barrier, 10)
+    go(kv_ways)
+    for weight in range(4):
+        go(along[weight])
+
+    def at_step(step, hooks):
+        for when, event in hooks:
+            pl.when(step == when)(event)
+
+    def events(*calls):
+        def run():
+            for call, *arguments in calls:
+                call(*arguments)
+
+        return run
 
     own = pl.ds(rank * 2, 2)
     copies = [
@@ -378,8 +441,8 @@
     def vector_row(index):
         return vec[index : index + 1, :]
 
-    keep_zero = keep_ref[0, 0].astype(F32) / KEEP_RATE
-    keep_one = keep_ref[1, 0].astype(F32) / KEEP_RATE
+    keep_zero = keep_ref[0, 2 * rank].astype(F32) / KEEP_RATE
+    keep_one = keep_ref[0, 2 * rank + 1].astype(F32) / KEEP_RATE
     lane_wide = lambda value: jnp.concatenate([value] * 3, axis=1)
     big_factor = lane_wide(jnp.where((sub & 2) == 0, keep_zero, keep_one))
     small_factor = lane_wide(jnp.where((sub & 1) == 0, keep_zero, keep_one))
@@ -395,7 +458,7 @@
             pad_big[rows_at((micro * 14 + h) * 32, 28), :] = xb_raw[micro, h].astype(F32).reshape(28, C)
             return 0
 
-        lax.fori_loop(0, 14, put_big, 0)
+        unrolled(14, put_big)
         for p in range(7):
             start = p * 32 + micro * 16
             g_wide[start : start + 14, :] = gb_raw[micro, p].astype(F32).reshape(14, C2)
@@ -407,13 +470,16 @@
             start = BLOCK_BIG + (unit * 3 + p) * 16
             g_wide[start : start + 16, :] = nn(pick_small, source.astype(BF16))
 
+    arrived(kv_ways)
+    go(kv_twin)
+
     def spread_rows(hh, _):
         tiles = [pad_big[rows_at((micro * 14 + half * 7 + hh) * 32, 32), :] for half in range(2) for micro in range(2)]
         source = jnp.concatenate(tiles, axis=0).astype(BF16)
         halo_big[rows_at((hh + 3) * 112, 112), :] = nn(spread_big, source)
         return 0
 
-    lax.fori_loop(0, BIG_HALF, spread_rows, 0)
+    unrolled(BIG_HALF, spread_rows)
     for unit in range(UNITS):
         def spread_unit(hh, _):
             tiles = [
@@ -423,7 +489,7 @@
             halo_small[rows_at(unit * HALO_SMALL + (hh + 3) * 48, 48), :] = nn(spread_small, source)
             return 0
 
-        lax.fori_loop(0, SMALL_HALF, spread_unit, 0)
+        unrolled(SMALL_HALF, spread_unit)
 
     def halos(ref, base, half, side):
         def step(index, _):
@@ -435,7 +501,7 @@
                 ref[rows_at(base + index * 8, 8), lanes] = pltpu.roll(high, 4, 0) * bottom
             return 0
 
-        lax.fori_loop(0, 3 * side, step, 0)
+        unrolled(3 * side, step)
 
     def all_halos(big, small):
         halos(big, 0, BIG_HALF, BIG_SIDE)
@@ -444,21 +510,20 @@
 
     all_halos(halo_big, halo_small)
 
-    kv_way = gather_core(kv_all, kv_way)
-    arrived(kv_way)
+    arrived(kv_twin)
     kv = jnp.transpose(flat(kv_all[...]).astype(F32))
     vec[...] = kv[64:80]
     for tap in range(TAPS):
         taps[tap] = jnp.broadcast_to(kv[tap : tap + 1] * (1.0 / KS), (8, C))
 
-    def convolve(big, small, mirrored, finish, between):
+    def convolve(big, small, mirrored, finish, hooks):
         def tap_at(i, j, lanes):
             index = i * KS + j
             return taps[TAPS - 1 - index if mirrored else index, :, lanes]
 
-        def row(step, _):
+        def image_row(step, _):
             h, lane = step // 3, lax.rem(step, 3)
-            lanes = pl.ds(pl.multiple_of(lane * 128, 128), 128)
+            lanes = pl.ds(aligned(lane * 128, 128), 128)
             sums = [None] * BIG_SIDE
             for i in range(KS):
                 values = [big[rows_at(((h + i) * BIG_SIDE + w) * 8, 8), lanes] for w in range(BIG_SIDE)]
@@ -469,14 +534,14 @@
                         sums[w] = term if sums[w] is None else sums[w] + term
             for w in range(BIG_SIDE):
                 finish((h * BIG_SIDE + w) * 8, sums[w], lanes)
+            at_step(step, hooks)
             return 0
 
-        lax.fori_loop(0, BIG_HALF * 3, row, 0)
-        between()
+        lax.fori_loop(0, BIG_HALF * 3, image_row, 0)
 
         def small_row(step, _):
             h, lane = step // 3, lax.rem(step, 3)
-            lanes = pl.ds(pl.multiple_of(lane * 128, 128), 128)
+            lanes = pl.ds(aligned(lane * 128, 128), 128)
             sums = [[None] * SMALL_SIDE for _ in range(UNITS)]
             for i in range(KS):
                 values = [
@@ -503,30 +568,21 @@
     def keep_conv(start, value, lanes):
         conv[rows_at(start, 8), lanes] = value
 
-    ways = {}
-    up_way = gather_plane(up_all, up_way)
-    ways["down"] = down_way
-    ways["strided"] = strided_way
-
-    def weights_on():
-        ways["down"] = gather_plane(down_all, ways["down"])
-        ways["strided"] = gather_plane(strided_all, ways["strided"])
-        ways["up"] = gather_core(up_all, up_way)
-
-    convolve(halo_big, halo_small, False, keep_conv, weights_on)
+    convolve(halo_big, halo_small, False, keep_conv, [(3, events((pass_line, 0))), (20, events((pass_line, 1)))])
+    pass_plane(0)
 
     def for_tiles(run):
         def big_tile(index, _):
             run(index * 112, 112, big_factor, halo_big, dhalo_big, 336 + index * 112)
             return 0
 
-        lax.fori_loop(0, BIG_HALF, big_tile, 0)
+        unrolled(BIG_HALF, big_tile)
 
         def small_tile(index, _):
             run(BIG_ROWS + index * 144, 144, small_factor, halo_small, dhalo_small, index * HALO_SMALL + 144)
             return 0
 
-        lax.fori_loop(0, UNITS, small_tile, 0)
+        unrolled(UNITS, small_tile)
 
     def fold(value):
         return jnp.sum(value.reshape(-1, 8, value.shape[-1]), axis=0)
@@ -546,41 +602,42 @@
         unit = centered * scale
         conv[rows, :] = unit
         rstd_one[rows, :] = jnp.broadcast_to(scale, (size, 128))
-        normed[pl.ds(pl.multiple_of(start, 16), size), :] = (
+        normed[pl.ds(aligned(start, 16), size), :] = (
             unit * vector_row(V_GAIN_ONE) + vector_row(V_OFFSET_ONE)
         ).astype(BF16)
 
     for_tiles(norm_one)
+    pass_line(2)
 
     def up_tile(index, _):
-        rows = pl.ds(pl.multiple_of(index * TILE, 16), TILE)
+        rows = pl.ds(aligned(index * TILE, 16), TILE)
         left = normed[rows, :]
         for chunk in range(FF // CHUNK):
             span = slice(chunk * CHUNK, (chunk + 1) * CHUNK)
             bias = vector_row(V_BIAS_UP + chunk)
             pre = (
-                lax.dot_general(left, flat(up_all[chunk]), (((1,), (1,)), ((), ())), preferred_element_type=F32)
+                lax.dot_general(left, flat(w_all[0, chunk]), (((1,), (1,)), ((), ())), preferred_element_type=F32)
                 * UP_SCALE
                 + bias
             )
-            whole = 0.5 + 0.5 * lax.erf(pre * math.sqrt(0.5))
-            density = jnp.exp(pre * pre * -0.5) * (1.0 / math.sqrt(2.0 * math.pi))
+            scaled_pre = pre * math.sqrt(0.5)
+            whole = 0.5 + 0.5 * lax.erf(scaled_pre)
+            density = jnp.exp2(scaled_pre * scaled_pre * -math.log2(math.e))
             hidden[rows, span] = (pre * whole).astype(BF16)
-            slope[rows, span] = whole + pre * density
+            slope[rows, span] = whole + pre * density * (1.0 / math.sqrt(2.0 * math.pi))
+        at_step(index, [(0, events((pass_line, 3))), (2, events((pass_plane, 1)))])
         return 0
 
-    arrived(ways["up"])
+    held(0)
     lax.fori_loop(0, ROWS // TILE, up_tile, 0)
-    ways["down"] = gather_core(down_all, ways["down"])
-    arrived(ways["down"])
+    held(1)
 
     def branch_tile(index, _):
-        rows = pl.ds(pl.multiple_of(index * TILE, 16), TILE)
-        branch[rows, :] = nn(hidden[rows, :], flat(down_all[...])) * DOWN_SCALE + vector_row(V_BIAS_DOWN)
+        rows = pl.ds(aligned(index * TILE, 16), TILE)
+        branch[rows, :] = nn(hidden[rows, :], flat(w_all[1])) * DOWN_SCALE + vector_row(V_BIAS_DOWN)
         return 0
 
     lax.fori_loop(0, ROWS // TILE, branch_tile, 0)
-    ways["strided"] = gather_core(strided_all, ways["strided"])
 
     def scaled(value, factor):
         return (value.reshape(-1, 8, C) * factor[None]).reshape(-1, C)
@@ -593,7 +650,7 @@
         unit = centered * scale
         xhat[rows, :] = unit
         rstd_two[rows, :] = jnp.broadcast_to(scale, (size, 128))
-        zeta[pl.ds(pl.multiple_of(start, 16), size), :] = (
+        zeta[pl.ds(aligned(start, 16), size), :] = (
             unit * vector_row(V_GAIN_TWO) + vector_row(V_OFFSET_TWO)
         ).astype(BF16)
 
@@ -602,11 +659,11 @@
     def block_spans(base, count, hh, half_side):
         for half in range(2):
             h = half * half_side + hh
-            p, a = h // 2, lax.rem(h, 2)
+            p, a = h // 2, h % 2
             for b in range(2):
                 yield (
-                    pl.ds(pl.multiple_of(base + p * count, 16), count),
-                    pl.ds(pl.multiple_of((2 * a + b) * C, 128), C),
+                    pl.ds(aligned(base + p * count, 16), count),
+                    pl.ds(aligned((2 * a + b) * C, 128), C),
                 )
 
     def block_rows(source, matrix, base, count, hh, half_side):
@@ -615,75 +672,74 @@
             blocks[span] = picked[index * count : (index + 1) * count]
 
     def big_blocks(hh, _):
-        block_rows(zeta[pl.ds(pl.multiple_of(hh * 112, 16), 112), :], block_big, 0, 32, hh, 7)
+        block_rows(zeta[pl.ds(aligned(hh * 112, 16), 112), :], block_big, 0, 32, hh, 7)
         return 0
 
-    lax.fori_loop(0, BIG_HALF, big_blocks, 0)
+    unrolled(BIG_HALF, big_blocks)
     for unit in range(UNITS):
         def small_blocks(hh, _):
-            source = zeta[pl.ds(pl.multiple_of(BIG_ROWS + unit * SMALL_ROWS + hh * 48, 16), 48), :]
+            source = zeta[pl.ds(aligned(BIG_ROWS + unit * SMALL_ROWS + hh * 48, 16), 48), :]
             block_rows(source, block_small, BLOCK_BIG + unit * 48, 16, hh, 3)
             return 0
 
-        lax.fori_loop(0, SMALL_HALF, small_blocks, 0)
+        unrolled(SMALL_HALF, small_blocks)
 
     g_rows[...] = g_wide[...].astype(BF16)
     bias_out_grad = jnp.sum(g_wide[...], axis=0, keepdims=True)
     d_vec[V_BIAS_OUT, 0:1, :] = bias_out_grad[:, :C]
     d_vec[V_BIAS_OUT + 1, 0:1, :] = bias_out_grad[:, C:]
 
-    def strided_grad(index, _):
-        span = pl.ds(pl.multiple_of(index * C, 128), C)
-        d_strided[index] = (
-            (
-                lax.dot_general(blocks[:, span], g_rows[...], (((0,), (0,)), ((), ())), preferred_element_type=F32)
-                * STRIDED_SCALE
+    def outer(left, right, scale):
+        product = lax.dot_general(left, right, (((0,), (0,)), ((), ())), preferred_element_type=F32)
+        return (product * scale).astype(BF16).reshape(2, 2, 2, PIECE, C)
+
+    for half in range(2):
+        def strided_grad(index, _):
+            span = pl.ds(aligned(index * C, 128), C)
+            d_all[2 + half, index] = outer(blocks[:, span], g_rows[:, half * C : half * C + C], STRIDED_SCALE)
+            return 0
+
+        lax.fori_loop(0, 4, strided_grad, 0)
+        go(red_core[2 + half])
+        if half == 0:
+            pass_plane(2)
+
+    bias_out = jnp.concatenate([vector_row(V_BIAS_OUT), vector_row(V_BIAS_OUT + 1)], axis=1)
+
+    def out_half(half):
+        span = slice(half * C, half * C + C)
+        g_wide[:, span] = nn(blocks[...], flat(w_all[2 + half])) * STRIDED_SCALE + bias_out[:, span]
+
+    held(2)
+    out_half(0)
+    pass_plane(3)
+    held(3)
+
+    def block_grad(index, _):
+        span = pl.ds(aligned(index * 384, 128), 384)
+        total = None
+        for half in range(2):
+            term = lax.dot_general(
+                g_rows[:, half * C : half * C + C],
+                flat(w_all[2 + half, index]),
+                (((1,), (1,)), ((), ())),
+                preferred_element_type=F32,
             )
-            .astype(BF16)
-            .reshape(2, 192, C2)
-        )
+            total = term if total is None else total + term
+        d_blocks[:, span] = (total * STRIDED_SCALE).astype(BF16)
         return 0
 
-    lax.fori_loop(0, 4, strided_grad, 0)
-    ways["d_strided"] = reduce_core(d_strided, strided_core)
-    arrived(ways["strided"])
-
-    bias_out = jnp.concatenate([vector_row(V_BIAS_OUT), vector_row(V_BIAS_OUT + 1)], axis=1)
-
-    for chunk in range(3):
-        span = slice(chunk * 256, chunk * 256 + 256)
-        g_wide[:, span] = nn(blocks[...], flat(strided_all[:, :, :, span])) * STRIDED_SCALE + bias_out[:, span]
-    for micro in range(2):
-        for p in range(7):
-            start = p * 32 + micro * 16
-            out_big_ref[micro, p] = g_wide[start : start + 14, :].reshape(7, 2, C2)
-    for unit in range(UNITS):
-        for p in range(3):
-            for crop in range(2):
-                start = BLOCK_BIG + (unit * 3 + p) * 16 + crop * 8
-                out_small_ref[2 * unit + crop, p] = g_wide[start : start + 6, :].reshape(3, 2, C2)
-
-    def block_grad(index, _):
-        span = pl.ds(pl.multiple_of(index * 384, 128), 384)
-        blocks[:, span] = (
-            lax.dot_general(
-                g_rows[...], flat(strided_all[index]), (((1,), (1,)), ((), ())), preferred_element_type=F32
-            )
-            * STRIDED_SCALE
-        ).astype(BF16)
-        return 0
-
     lax.fori_loop(0, 4, block_grad, 0)
 
     def unblock(matrix, base, count, hh, half_side):
-        parts = jnp.concatenate([blocks[span] for span in block_spans(base, count, hh, half_side)], axis=0)
+        parts = jnp.concatenate([d_blocks[span] for span in block_spans(base, count, hh, half_side)], axis=0)
         return lax.dot_general(matrix, parts, (((0,), (0,)), ((), ())), preferred_element_type=F32)
 
     def big_unblock(hh, _):
         d_zeta[rows_at(hh * 112, 112), :] = unblock(block_big, 0, 32, hh, 7)
         return 0
 
-    lax.fori_loop(0, BIG_HALF, big_unblock, 0)
+    unrolled(BIG_HALF, big_unblock)
     for unit in range(UNITS):
         def small_unblock(hh, _):
             d_zeta[rows_at(BIG_ROWS + unit * SMALL_ROWS + hh * 48, 48), :] = unblock(
@@ -691,9 +747,9 @@
             )
             return 0
 
-        lax.fori_loop(0, SMALL_HALF, small_unblock, 0)
-
-    ways["d_strided"] = reduce_plane(d_strided, strided_core, strided_plane, ways["d_strided"])
+        unrolled(SMALL_HALF, small_unblock)
+
+    sum_core(2)
 
     for index in range(11):
         d_vec[index] = jnp.zeros((8, C), F32)
@@ -710,54 +766,52 @@
         kept = scaled(mixed, factor)
         d_vec[V_SCALE] += fold(kept * branch[rows, :])
         lowered = (kept * vector_row(V_SCALE)).astype(BF16)
-        d_branch[pl.ds(pl.multiple_of(start, 16), size), :] = lowered
+        d_branch[pl.ds(aligned(start, 16), size), :] = lowered
         d_vec[V_BIAS_DOWN] += fold(lowered.astype(F32))
 
     for_tiles(norm_two_back)
+    sum_core(3)
+
+    def down_grad(index, _):
+        span = pl.ds(aligned(index * C, 128), C)
+        d_all[1, index] = outer(hidden[:, span], d_branch[...], DOWN_SCALE)
+        return 0
+
+    lax.fori_loop(0, 4, down_grad, 0)
+    go(red_core[1])
 
     d_bias_up[...] = jnp.zeros_like(d_bias_up)
 
     def down_tile(index, _):
-        rows = pl.ds(pl.multiple_of(index * TILE, 16), TILE)
+        rows = pl.ds(aligned(index * TILE, 16), TILE)
         left = d_branch[rows, :]
         for chunk in range(FF // CHUNK):
             span = slice(chunk * CHUNK, (chunk + 1) * CHUNK)
             d_hidden = (
-                lax.dot_general(left, flat(down_all[chunk]), (((1,), (1,)), ((), ())), preferred_element_type=F32)
+                lax.dot_general(left, flat(w_all[1, chunk]), (((1,), (1,)), ((), ())), preferred_element_type=F32)
                 * DOWN_SCALE
             )
             lowered = (d_hidden * slope[rows, span]).astype(BF16)
             d_pre[rows, span] = lowered
             d_bias_up[:, span] += fold(lowered.astype(F32))
-        d_normed[rows, :] = (nn(d_pre[rows, :], flat(up_all[...])) * UP_SCALE).astype(BF16)
+        d_normed[rows, :] = (nn(d_pre[rows, :], flat(w_all[0])) * UP_SCALE).astype(BF16)
+        at_step(index, [(2, events((sum_core, 1))), (3, events((sum_plane, 2)))])
         return 0
 
     lax.fori_loop(0, ROWS // TILE, down_tile, 0)
 
-    def outer(left, right, scale):
-        product = lax.dot_general(left, right, (((0,), (0,)), ((), ())), preferred_element_type=F32)
-        return (product * scale).astype(BF16).reshape(2, 192, C)
-
-    def down_grad(index, _):
-        span = pl.ds(pl.multiple_of(index * C, 128), C)
-        d_down[index] = outer(hidden[:, span], d_branch[...], DOWN_SCALE)
+    def up_grad(index, _):
+        span = pl.ds(aligned(index * C, 128), C)
+        d_all[0, index] = outer(d_pre[:, span], normed[...], UP_SCALE)
         return 0
 
-    def up_grad(index, _):
-        span = pl.ds(pl.multiple_of(index * C, 128), C)
-        d_up[index] = outer(d_pre[:, span], normed[...], UP_SCALE)
-        return 0
-
-    lax.fori_loop(0, 4, down_grad, 0)
-    ways["d_down"] = reduce_core(d_down, down_core)
     lax.fori_loop(0, 4, up_grad, 0)
-    ways["d_up"] = reduce_core(d_up, up_core)
-    ways["d_down"] = reduce_plane(d_down, down_core, down_plane, ways["d_down"])
+    go(red_core[0])
 
     def norm_one_back(start, size, _, __, target, offset):
         rows = rows_at(start, size)
         unit = conv[rows, :]
-        grad = d_normed[pl.ds(pl.multiple_of(start, 16), size), :].astype(F32)
+        grad = d_normed[pl.ds(aligned(start, 16), size), :].astype(F32)
         d_vec[V_GAIN_ONE] += fold(grad * unit)
         d_vec[V_OFFSET_ONE] += fold(grad)
         inner = grad * vector_row(V_GAIN_ONE)
@@ -766,50 +820,47 @@
         target[rows_at(offset, size), :] = result
 
     for_tiles(norm_one_back)
-    ways["d_up"] = reduce_plane(d_up, up_core, up_plane, ways["d_up"])
-    ways["d_strided"] = reduce_line(strided_core, strided_plane, strided_line, ways["d_strided"])
     all_halos(dhalo_big, dhalo_small)
 
     def tap_grads(step, _):
         i, lane = step // 3, lax.rem(step, 3)
-        lanes = pl.ds(pl.multiple_of(lane * 128, 128), 128)
-
-        def image_row(side, field, grad, field_base, grad_base, sums):
+        lanes = pl.ds(aligned(lane * 128, 128), 128)
+
+        sums = [[None, None] for _ in range(KS)]
+
+        def image_row(side, field, grad, field_base, grad_base, turn):
             inputs = [field[rows_at(field_base + w * 8, 8), lanes] for w in range(side)]
             outer = [grad[rows_at(grad_base + w * 8, 8), lanes] for w in range(side)]
-            result = []
-            for j in range(KS):
-                total = sums[j]
-                for w in range(max(0, 3 - j), min(side, side + 3 - j)):
-                    total = total + inputs[w + j - 3] * outer[w]
-                result.append(total)
-            return tuple(result)
-
-        sums = tuple(jnp.zeros((8, 128), F32) for _ in range(KS))
-        sums = lax.fori_loop(
-            0,
-            BIG_HALF,
-            lambda h, carry: image_row(
-                BIG_SIDE, halo_big, dhalo_big, (h + i) * 112, (h + 3) * 112, carry
-            ),
-            sums,
+            for w in range(side):
+                for j in range(max(0, 3 - w), min(KS, side + 3 - w)):
+                    term = inputs[w + j - 3] * outer[w]
+                    slot = (w + turn) % 2
+                    old = sums[j][slot]
+                    sums[j][slot] = term if old is None else old + term
+
+        for h in range(BIG_HALF):
+            image_row(BIG_SIDE, halo_big, dhalo_big, (h + i) * 112, (h + 3) * 112, h)
+        for h in range(SMALL_HALF):
+            for unit in range(UNITS):
+                base = unit * HALO_SMALL
+                image_row(SMALL_SIDE, halo_small, dhalo_small, base + (h + i) * 48, base + (h + 3) * 48, h)
+        for j in range(KS):
+            d_taps[i * KS + j, :, lanes] = sums[j][0] + sums[j][1]
+        at_step(
+            step,
+            [
+                (3, events((sum_plane, 3))),
+                (5, events((sum_core, 0))),
+                (7, events((sum_line, 2))),
+                (16, events((sum_line, 3))),
+                (19, events((sum_plane, 1))),
+            ],
         )
-        for unit in range(UNITS):
-            sums = lax.fori_loop(
-                0,
-                SMALL_HALF,
-                lambda h, carry, base=unit * HALO_SMALL: image_row(
-                    SMALL_SIDE, halo_small, dhalo_small, base + (h + i) * 48, base + (h + 3) * 48, carry
-                ),
-                sums,
-            )
-        for j in range(KS):
-            d_taps[i * KS + j, :, lanes] = sums[j]
         return 0
 
     lax.fori_loop(0, KS * 3, tap_grads, 0)
 
-    d_kv[56:64, :] = jnp.zeros((8, C), F32)
+    d_kv[56:128, :] = jnp.zeros((72, C), F32)
     for tap in range(TAPS):
         d_kv[tap : tap + 1, :] = jnp.sum(d_taps[tap], axis=0, keepdims=True) * (1.0 / KS)
     for index in range(11):
@@ -824,42 +875,35 @@
             :, index * C : (index + 1) * C
         ]
 
-    ways["d_kv"] = [send(d_kv, kv_core, twin)]
-
-    def kv_rows(index):
-        return pl.ds(pl.multiple_of(index * 16, 16), 16)
-
-    def kv_reduce_plane(copies):
-        arrived(copies)
-        kv_core[...] += d_kv[...]
-        return [send(kv_core.at[kv_rows(flanks[index])], kv_plane.at[index], on_plane(index)) for index in range(3)]
-
-    def kv_reduce_line(copies):
-        arrived(copies)
-        kv_line[0] = kv_core[kv_rows(rank), :] + kv_plane[0] + kv_plane[1] + kv_plane[2]
-        return [send(kv_line.at[0], kv_line.at[offset], on_line(offset)) for offset in (1, 2, 3)]
-
-    def kv_reduce_back(copies):
-        arrived(copies)
-        total = jnp.zeros((16, C), F32)
-        for index in range(PLANES):
-            total = total + kv_line[lax.rem(line - index + PLANES, PLANES)]
-        kv_sum[kv_rows(rank), :] = total
-        part = kv_sum.at[kv_rows(rank)]
-        return [send(part, part, on_plane(index)) for index in range(3)]
+    kv_part[...] = jnp.transpose(d_kv[...]).astype(BF16).reshape(8, PIECE, 128)
+    go(kv_across)
 
     def add_grad(start, value, lanes):
         d_mixed[rows_at(start, 8), lanes] += value
 
-    def gradients_on():
-        ways["d_kv"] = kv_reduce_plane(ways["d_kv"])
-        ways["d_down"] = reduce_line(down_core, down_plane, down_line, ways["d_down"])
-        ways["d_strided"] = reduce_back(strided_line, strided_sum, ways["d_strided"])
-
-    convolve(dhalo_big, dhalo_small, True, add_grad, gradients_on)
-    ways["d_kv"] = kv_reduce_line(ways["d_kv"])
-    ways["d_up"] = reduce_line(up_core, up_plane, up_line, ways["d_up"])
-    ways["d_down"] = reduce_back(down_line, down_sum, ways["d_down"])
+    convolve(
+        dhalo_big,
+        dhalo_small,
+        True,
+        add_grad,
+        [
+            (14, events((sum_line, 1), (kv_sum_group,))),
+            (18, events((sum_plane, 0))),
+        ],
+    )
+    out_half(1)
+    for micro in range(2):
+        for p in range(7):
+            start = p * 32 + micro * 16
+            out_big_ref[micro, p] = g_wide[start : start + 14, :].reshape(7, 2, C2)
+    for unit in range(UNITS):
+        for p in range(3):
+            for crop in range(2):
+                start = BLOCK_BIG + (unit * 3 + p) * 16 + crop * 8
+                out_small_ref[2 * unit + crop, p] = g_wide[start : start + 6, :].reshape(3, 2, C2)
+
+
+    sum_line(0)
 
     def restore(matrix, value):
         high = value.astype(BF16)
@@ -874,7 +918,7 @@
                 grad_big_ref[micro, half * 7 + hh] = natural[start : start + 28].reshape(14, 2, C)
         return 0
 
-    lax.fori_loop(0, BIG_HALF, grad_rows, 0)
+    unrolled(BIG_HALF, grad_rows)
     for unit in range(UNITS):
         def small_grad_rows(hh, _):
             natural = restore(gather_small, d_mixed[rows_at(BIG_ROWS + unit * SMALL_ROWS + hh * 48, 48), :])
@@ -884,22 +928,63 @@
                     grad_small_ref[2 * unit + crop, half * 3 + hh] = natural[start : start + 12].reshape(6, 2, C)
             return 0
 
-        lax.fori_loop(0, SMALL_HALF, small_grad_rows, 0)
-
-    ways["d_kv"] = kv_reduce_back(ways["d_kv"])
-    ways["d_up"] = reduce_back(up_line, up_sum, ways["d_up"])
-    for name, final, target in (
-        ("d_strided", strided_sum, strided_out),
-        ("d_down", down_sum, down_out),
-        ("d_up", up_sum, up_out),
-    ):
-        arrived(ways[name])
-        target[...] = final[...]
-    arrived(ways["d_kv"])
-    kv_turn[...] = jnp.transpose(kv_sum[...])
-    kv_out[...] = kv_turn[pl.ds(pl.multiple_of(dp_rank * PIECE, 16), PIECE), :]
-    for copy in pending:
+        unrolled(SMALL_HALF, small_grad_rows)
+
+    for weight in range(4):
+        arrived(red_back[weight])
+    up_out[...] = flat(final[0])
+    down_out[...] = flat(final[1])
+    strided_out[:, :C] = flat(final[2])
+    strided_out[:, C:] = flat(final[3])
+    arrived(kv_back)
+    kv_out[...] = kv_sum[0] + kv_sum[1] + kv_sum[2] + kv_sum[3]
+    for copy in made:
         copy.wait_send()
+
+
+def finish_kernel(rates, *refs):
+    d_kv, d_up, d_down, d_strided = refs[:4]
+    state, images, outs = refs[4:19], refs[19:23], refs[23:42]
+    held, sems = refs[42:46], refs[46]
+    inward = [pltpu.make_async_copy(images[index], held[index], sems.at[index]) for index in range(4)]
+    outward = [pltpu.make_async_copy(held[index], outs[index], sems.at[4 + index]) for index in range(4)]
+    for copy in inward:
+        copy.start()
+    for copy, onward in zip(inward, outward):
+        copy.wait()
+        onward.start()
+    packed = d_kv[...]
+    gradients = (
+        packed[:, :TAPS],
+        jnp.transpose(packed)[TAPS : TAPS + 13],
+        d_up[...].astype(F32),
+        d_down[...].astype(F32),
+        d_strided[...].astype(F32),
+    )
+    for position in range(5):
+        weight, moment, average = state[3 * position : 3 * position + 3]
+        new_weight, new_moment, new_average = outs[4 + 3 * position : 7 + 3 * position]
+        gradient = gradients[position]
+        moment_next = MOMENTUM * moment[...] + gradient
+        weight_next = weight[...] - rates[position] * (gradient + MOMENTUM * moment_next)
+        new_moment[...] = moment_next
+        new_weight[...] = weight_next
+        new_average[...] = AVERAGING * average[...] + (1.0 - AVERAGING) * weight_next
+    for copy in outward:
+        copy.wait()
+
+
+def finish(rates, grads, state, images):
+    any_spec = pl.BlockSpec(memory_space=pl.ANY)
+    vmem = pl.BlockSpec(memory_space=pltpu.VMEM)
+    return pl.pallas_call(
+        functools.partial(finish_kernel, rates),
+        out_shape=[jax.ShapeDtypeStruct(array.shape, F32) for array in (*images, *state)],
+        in_specs=[vmem] * 19 + [any_spec] * 4,
+        out_specs=[any_spec] * 4 + [vmem] * 15,
+        scratch_shapes=[pltpu.VMEM(array.shape, F32) for array in images] + [pltpu.SemaphoreType.DMA((8,))],
+        compiler_params=pltpu.CompilerParams(vmem_limit_bytes=(63 << 20) + (1 << 19)),
+    )(*grads, *state, *images)
 
 
 def fused_step(big_crops, small_crops, big_cot, small_cot, keep, kernel_t, vector, up_t, down, strided):
@@ -914,7 +999,7 @@
             shape((6, 3, 3, 2, C2), F32),
             shape((2, 14, 14, 2, C), F32),
             shape((6, 6, 6, 2, C), F32),
-            shape((PIECE, 64), F32),
+            shape((PIECE, 128), F32),
             shape((192, C), BF16),
             shape((192, C), BF16),
             shape((192, C2), BF16),
@@ -940,46 +1025,31 @@
             pltpu.VMEM((ROWS, 128), F32),
             pltpu.VMEM((ROWS, C), BF16),
             pltpu.VMEM((BLOCKS, 4 * C), BF16),
+            pltpu.VMEM((BLOCKS, 4 * C), BF16),
             pltpu.VMEM((BLOCKS, C2), F32),
             pltpu.VMEM((BLOCKS, C2), BF16),
-            pltpu.VMEM((ROWS, C), F32),
-            pltpu.VMEM((ROWS, C), F32),
             pltpu.VMEM((ROWS, C), BF16),
             pltpu.VMEM((ROWS, FF), BF16),
-            pltpu.VMEM((ROWS, C), BF16),
             pltpu.VMEM((HALO_BIG, C), F32),
             pltpu.VMEM((UNITS * HALO_SMALL, C), F32),
             pltpu.VMEM((TAPS, 8, C), F32),
             pltpu.VMEM((13, 8, C), F32),
             pltpu.VMEM((8, FF), F32),
             pltpu.VMEM((4, 2, 48, 128), BF16),
-            pltpu.VMEM((4, 2, 192, C), BF16),
-            pltpu.VMEM((4, 2, 192, C), BF16),
-            pltpu.VMEM((4, 2, 192, C2), BF16),
-            pltpu.VMEM((4, 2, 192, C), BF16),
-            pltpu.VMEM((4, 2, 192, C), BF16),
-            pltpu.VMEM((4, 2, 192, C2), BF16),
-            pltpu.VMEM((4, 192, C), BF16),
-            pltpu.VMEM((4, 192, C), BF16),
-            pltpu.VMEM((4, 192, C2), BF16),
-            pltpu.VMEM((3, 4, PIECE, C), BF16),
-            pltpu.VMEM((3, 4, PIECE, C), BF16),
-            pltpu.VMEM((3, 4, PIECE, C2), BF16),
-            pltpu.VMEM((7, PIECE, C), BF16),
-            pltpu.VMEM((7, PIECE, C), BF16),
-            pltpu.VMEM((7, PIECE, C2), BF16),
-            pltpu.VMEM((192, C), BF16),
-            pltpu.VMEM((192, C), BF16),
-            pltpu.VMEM((192, C2), BF16),
-            pltpu.VMEM((64, C), F32),
-            pltpu.VMEM((64, C), F32),
-            pltpu.VMEM((3, 16, C), F32),
-            pltpu.VMEM((4, 16, C), F32),
-            pltpu.VMEM((64, C), F32),
-            pltpu.VMEM((C, 64), F32),
+            pltpu.VMEM((4, 4, 2, 192, C), BF16),
+            pltpu.VMEM((4, 4, 2, 2, 2, PIECE, C), BF16),
+            pltpu.VMEM((4, 4, 2, 2, PIECE, C), BF16),
+            pltpu.VMEM((4, 3, 4, PIECE, C), BF16),
+            pltpu.VMEM((4, 4, PIECE, C), BF16),
+            pltpu.VMEM((4, 3, PIECE, C), BF16),
+            pltpu.VMEM((4, 4, PIECE, C), BF16),
+            pltpu.VMEM((128, C), F32),
+            pltpu.VMEM((8, PIECE, 128), BF16),
+            pltpu.VMEM((7, PIECE, 128), BF16),
+            pltpu.VMEM((4, PIECE, 128), F32),
             pltpu.SemaphoreType.DMA((4,)),
-            pltpu.SemaphoreType.DMA((83,)),
-            pltpu.SemaphoreType.DMA((83,)),
+            pltpu.SemaphoreType.DMA((COPIES,)),
+            pltpu.SemaphoreType.DMA((COPIES,)),
         ],
         compiler_params=pltpu.CompilerParams(vmem_limit_bytes=(63 << 20) + (1 << 19), collective_id=0, has_side_effects=True),
     )(
@@ -994,14 +1064,7 @@
         down,
         strided,
     )
-    back_big, back_small = (0, 3, 1, 2, 4), (3, 0, 1, 2, 4)
-    return (
-        results[0].transpose(back_big),
-        results[1].transpose(back_small),
-        results[2].transpose(back_big),
-        results[3].transpose(back_small),
-        *results[4:],
-    )
+    return results[4:], results[:4]
 
 
 def body(big_crops, small_crops, big_cot, small_cot, drop_mask, *state):
@@ -1022,31 +1085,23 @@
         [jnp.transpose(array) if turn else array for array, turn in zip(group, turned)]
         for group in (masters, moments, averages)
     )
-    keep = lax.dynamic_slice_in_dim(drop_mask, rank * 2, 2, 0)
-    out_big, out_small, grad_big, grad_small, d_kv, d_up, d_down, d_strided = fused_step(
-        big_crops, small_crops, big_cot, small_cot, keep, *masters
-    )
-    gradients = (
-        d_kv[:, :TAPS],
-        jnp.transpose(d_kv[:, TAPS : TAPS + masters[1].shape[0]]),
-        d_up.astype(F32),
-        d_down.astype(F32),
-        d_strided.astype(F32),
-    )
+    grads, images = fused_step(big_crops, small_crops, big_cot, small_cot, drop_mask.T, *masters)
     pixel_total = (
         lax.axis_size("dp")
         * micro_count
         * (math.prod(big_crops.shape[1:4]) + math.prod(small_crops.shape[1:4]))
     )
-    updates = []
-    for position in range(5):
-        step_rate = RATES[position] * math.sqrt(FANS[position] / pixel_total)
-        moment_next = MOMENTUM * moments[position] + gradients[position]
-        weight_next = masters[position] - step_rate * (gradients[position] + MOMENTUM * moment_next)
-        average_next = AVERAGING * averages[position] + (1.0 - AVERAGING) * weight_next
-        new = (weight_next, moment_next, average_next)
-        updates += [jnp.transpose(array) if turned[position] else array for array in new]
-    return (out_big, out_small, grad_big, grad_small, *updates)
+    rates = tuple(rate * math.sqrt(fan / pixel_total) for rate, fan in zip(RATES, FANS))
+    state = [array for group in zip(masters, moments, averages) for array in group]
+    results = finish(rates, grads, state, images)
+    order_big, order_small = (0, 3, 1, 2, 4), (3, 0, 1, 2, 4)
+    return (
+        results[0].transpose(order_big),
+        results[1].transpose(order_small),
+        results[2].transpose(order_big),
+        results[3].transpose(order_small),
+        *(array.T if turned[index // 3] else array for index, array in enumerate(results[4:])),
+    )
 
 
 def solution(mesh):

time: 118 us -> 94.4 us (0.80)
  local copies, waits for them, and re-layouts: 9.69 us -> 0 us
  Pallas kernels: 101 us -> 93.3 us
  other arithmetic: 6.36 us -> 0 us
    pallas_call x1, Pallas kernels: 101 us -> 86.3 us  [fused_step(): pl.pallas_call(step_kernel, out_shape=(shape((2, 7, 7, 2, C2), F32), shap...]
    unnamed x37 -> x0, local copies, waits for them, and re-layouts: 9.62 us -> none
    pallas_call x0 -> x1, Pallas kernels: none -> 7.06 us  [finish(): pl.pallas_call(functools.partial(finish_kernel, rates), out_shape=[jax.Sh...]
    transpose x2 -> x0, other arithmetic: 4.2 us -> none  [body(): jnp.transpose(array)]
    add x2 -> x0, other arithmetic: 2.16 us -> none  [body(): AVERAGING * averages[position] + (1.0 - AVERAGING) * weight_next]
where the time goes in v2:
time: 94.4 us; the launch traced here: 94.2 us
  Pallas kernels  93.3 us (99%)
    pallas_call x1, Pallas kernels, fused_step(): pl.pallas_call(step_kernel, out_shape=(shape((2, 7, 7, 2, C2), F32), shap...  86.3 us
    pallas_call x1, Pallas kernels, finish(): pl.pallas_call(functools.partial(finish_kernel, rates), out_shape=[jax.Sh...  7.06 us

profile of v2, /device:TPU:0, one launch (start us, length us, event | category | flops | bytes accessed | tf_op | source)
XLA Modules:
  0.0 94.2 jit_solution(14065346687269978979)
XLA Ops:
  0.7 86.3 %shard_map.339 = (f32[2,7,7,2,768]{4,3,2,1,0:T(2,128)}, f32[6,3,3,2,768]{4,3,2,1,0:T(2,128)}, f32[2,14,14,2,384]{4,3,2,1,0:T(2,128)}, f32[6,6,6,2,384]{4,3,2,1,0...) custom-call(bf16[8,14,14,2,384]{4,3,2,1,0:T(2,128)(2,1)} %bitcast.21, ...), custom_call_target="tpu_custom_call" | custom-call | tf_op jit(solution)/shard_map/pallas_call | solution.py:995
  87.0 7.1 %shard_map.340 = (f32[2,7,7,2,768]{4,3,2,1,0:T(2,128)}, f32[6,3,3,2,768]{4,3,2,1,0:T(2,128)}, f32[2,14,14,2,384]{4,3,2,1,0:T(2,128)}, f32[6,6,6,2,384]{4,3,2,1,0...) custom-call(f32[48,128]{1,0:T(8,128)} %get-tuple-element.46.refs_0_,, ...), custom_call_target="tpu_custom_call" | custom-call | tf_op jit(solution)/shard_map/pallas_call | solution.py:980

commit v3 on v2

--- a/solution.py
+++ b/solution.py
@@ -239,7 +239,8 @@
 
 def step_kernel(
     big_hbm, small_hbm, big_cot_hbm, small_cot_hbm, keep_ref, kernel_ref, vector_ref, up_shard, down_shard, strided_shard,
-    out_big_ref, out_small_ref, grad_big_ref, grad_small_ref, kv_out, up_out, down_out, strided_out,
+    out_big_hbm, out_small_hbm, grad_big_hbm, grad_small_hbm, kv_out, up_out, down_out, strided_out,
+    out_big_ref, out_small_ref, grad_big_ref, grad_small_ref,
     xb_raw, xs_raw, gb_raw, gs_raw, halo_big, halo_small, taps, vec, conv, rstd_one, normed,
     hidden, slope, branch, xhat, rstd_two, zeta, blocks, d_blocks, g_wide, g_rows, d_branch, d_pre,
     dhalo_big, dhalo_small, d_taps, d_vec, d_bias_up,
@@ -699,7 +700,7 @@
             d_all[2 + half, index] = outer(blocks[:, span], g_rows[:, half * C : half * C + C], STRIDED_SCALE)
             return 0
 
-        lax.fori_loop(0, 4, strided_grad, 0)
+        unrolled(4, strided_grad)
         go(red_core[2 + half])
         if half == 0:
             pass_plane(2)
@@ -729,7 +730,7 @@
         d_blocks[:, span] = (total * STRIDED_SCALE).astype(BF16)
         return 0
 
-    lax.fori_loop(0, 4, block_grad, 0)
+    unrolled(4, block_grad)
 
     def unblock(matrix, base, count, hh, half_side):
         parts = jnp.concatenate([d_blocks[span] for span in block_spans(base, count, hh, half_side)], axis=0)
@@ -777,7 +778,7 @@
         d_all[1, index] = outer(hidden[:, span], d_branch[...], DOWN_SCALE)
         return 0
 
-    lax.fori_loop(0, 4, down_grad, 0)
+    unrolled(4, down_grad)
     go(red_core[1])
 
     d_bias_up[...] = jnp.zeros_like(d_bias_up)
@@ -805,7 +806,7 @@
         d_all[0, index] = outer(d_pre[:, span], normed[...], UP_SCALE)
         return 0
 
-    lax.fori_loop(0, 4, up_grad, 0)
+    unrolled(4, up_grad)
     go(red_core[0])
 
     def norm_one_back(start, size, _, __, target, offset):
@@ -930,6 +931,19 @@
 
         unrolled(SMALL_HALF, small_grad_rows)
 
+    leaving = [
+        pltpu.make_async_copy(source, target, sems.at[4 + index])
+        for index, (source, target) in enumerate(
+            (
+                (out_big_ref, out_big_hbm),
+                (out_small_ref, out_small_hbm),
+                (grad_big_ref, grad_big_hbm),
+                (grad_small_ref, grad_small_hbm),
+            )
+        )
+    ]
+    for copy in leaving:
+        copy.start()
     for weight in range(4):
         arrived(red_back[weight])
     up_out[...] = flat(final[0])
@@ -940,51 +954,69 @@
     kv_out[...] = kv_sum[0] + kv_sum[1] + kv_sum[2] + kv_sum[3]
     for copy in made:
         copy.wait_send()
+    for copy in leaving:
+        copy.wait()
 
 
 def finish_kernel(rates, *refs):
-    d_kv, d_up, d_down, d_strided = refs[:4]
-    state, images, outs = refs[4:19], refs[19:23], refs[23:42]
-    held, sems = refs[42:46], refs[46]
-    inward = [pltpu.make_async_copy(images[index], held[index], sems.at[index]) for index in range(4)]
-    outward = [pltpu.make_async_copy(held[index], outs[index], sems.at[4 + index]) for index in range(4)]
-    for copy in inward:
-        copy.start()
-    for copy, onward in zip(inward, outward):
-        copy.wait()
-        onward.start()
-    packed = d_kv[...]
-    gradients = (
-        packed[:, :TAPS],
-        jnp.transpose(packed)[TAPS : TAPS + 13],
-        d_up[...].astype(F32),
-        d_down[...].astype(F32),
-        d_strided[...].astype(F32),
-    )
-    for position in range(5):
-        weight, moment, average = state[3 * position : 3 * position + 3]
-        new_weight, new_moment, new_average = outs[4 + 3 * position : 7 + 3 * position]
-        gradient = gradients[position]
-        moment_next = MOMENTUM * moment[...] + gradient
-        weight_next = weight[...] - rates[position] * (gradient + MOMENTUM * moment_next)
-        new_moment[...] = moment_next
-        new_weight[...] = weight_next
-        new_average[...] = AVERAGING * average[...] + (1.0 - AVERAGING) * weight_next
+    sources, outs, held, fresh, sems = refs[:23], refs[23:42], refs[42:65], refs[65:80], refs[80]
+    inward = [pltpu.make_async_copy(source, target, sems.at[index]) for index, (source, target) in enumerate(zip(sources, held))]
+    outward = [
+        pltpu.make_async_copy(source, target, sems.at[23 + index])
+        for index, (source, target) in enumerate(zip((*held[19:], *fresh), outs))
+    ]
+    order = (4, 3, 2, 1, 0)
+    for index in (19, 21):
+        inward[index].start()
+    for position in order:
+        if position:
+            inward[position - 1].start()
+        for index in range(4 + 3 * position, 7 + 3 * position):
+            inward[index].start()
+    for index in (20, 22):
+        inward[index].start()
+    for index in (19, 21):
+        inward[index].wait()
+        outward[index - 19].start()
+    for position in order:
+        state = range(4 + 3 * position, 7 + 3 * position)
+        for index in state:
+            inward[index].wait()
+        if position >= 2:
+            inward[position - 1].wait()
+            gradient = held[position - 1][...].astype(F32)
+        elif position == 1:
+            inward[0].wait()
+            gradient = jnp.transpose(held[0][...])[TAPS : TAPS + 13]
+        else:
+            gradient = held[0][:, :TAPS]
+        weight, moment, average = (held[index][...] for index in state)
+        moment_next = MOMENTUM * moment + gradient
+        weight_next = weight - rates[position] * (gradient + MOMENTUM * moment_next)
+        results = (weight_next, moment_next, AVERAGING * average + (1.0 - AVERAGING) * weight_next)
+        for index, value in enumerate(results):
+            fresh[3 * position + index][...] = value
+            outward[4 + 3 * position + index].start()
+    for index in (20, 22):
+        inward[index].wait()
+        outward[index - 19].start()
     for copy in outward:
         copy.wait()
 
 
 def finish(rates, grads, state, images):
     any_spec = pl.BlockSpec(memory_space=pl.ANY)
-    vmem = pl.BlockSpec(memory_space=pltpu.VMEM)
+    inputs = (*grads, *state, *images)
     return pl.pallas_call(
         functools.partial(finish_kernel, rates),
         out_shape=[jax.ShapeDtypeStruct(array.shape, F32) for array in (*images, *state)],
-        in_specs=[vmem] * 19 + [any_spec] * 4,
-        out_specs=[any_spec] * 4 + [vmem] * 15,
-        scratch_shapes=[pltpu.VMEM(array.shape, F32) for array in images] + [pltpu.SemaphoreType.DMA((8,))],
+        in_specs=[any_spec] * 23,
+        out_specs=[any_spec] * 19,
+        scratch_shapes=[pltpu.VMEM(array.shape, array.dtype) for array in inputs]
+        + [pltpu.VMEM(array.shape, F32) for array in state]
+        + [pltpu.SemaphoreType.DMA((42,))],
         compiler_params=pltpu.CompilerParams(vmem_limit_bytes=(63 << 20) + (1 << 19)),
-    )(*grads, *state, *images)
+    )(*inputs)
 
 
 def fused_step(big_crops, small_crops, big_cot, small_cot, keep, kernel_t, vector, up_t, down, strided):
@@ -1005,8 +1037,12 @@
             shape((192, C2), BF16),
         ),
         in_specs=[any_spec] * 4 + [pl.BlockSpec(memory_space=pltpu.SMEM)] + [vmem] * 5,
-        out_specs=[vmem] * 8,
+        out_specs=[any_spec] * 4 + [vmem] * 4,
         scratch_shapes=[
+            pltpu.VMEM((2, 7, 7, 2, C2), F32),
+            pltpu.VMEM((6, 3, 3, 2, C2), F32),
+            pltpu.VMEM((2, 14, 14, 2, C), F32),
+            pltpu.VMEM((6, 6, 6, 2, C), F32),
             pltpu.VMEM((2, 14, 14, 2, C), BF16),
             pltpu.VMEM((6, 6, 6, 8, C), BF16),
             pltpu.VMEM((2, 7, 7, 2, C2), BF16),
@@ -1047,7 +1083,7 @@
             pltpu.VMEM((8, PIECE, 128), BF16),
             pltpu.VMEM((7, PIECE, 128), BF16),
             pltpu.VMEM((4, PIECE, 128), F32),
-            pltpu.SemaphoreType.DMA((4,)),
+            pltpu.SemaphoreType.DMA((8,)),
             pltpu.SemaphoreType.DMA((COPIES,)),
             pltpu.SemaphoreType.DMA((COPIES,)),
         ],

time: 94.4 us -> 90.2 us (0.956)
  Pallas kernels: 93.3 us -> 89.2 us
    pallas_call x1, Pallas kernels: 86.3 us -> 83.3 us  [fused_step(): pl.pallas_call(step_kernel, out_shape=(shape((2, 7, 7, 2, C2), F32), shap...]
    pallas_call x1, Pallas kernels: 7.06 us -> 5.89 us  [finish(): pl.pallas_call(functools.partial(finish_kernel, rates), out_shape=[jax.Sh...]
where the time goes in v3:
time: 90.2 us; the launch traced here: 90 us
  Pallas kernels  89.2 us (99%)
    pallas_call x1, Pallas kernels, fused_step(): pl.pallas_call(step_kernel, out_shape=(shape((2, 7, 7, 2, C2), F32), shap...  83.3 us
    pallas_call x1, Pallas kernels, finish(): pl.pallas_call(functools.partial(finish_kernel, rates), out_shape=[jax.Sh...  5.89 us

profile of v3, /device:TPU:0, one launch (start us, length us, event | category | flops | bytes accessed | tf_op | source)
XLA Modules:
  0.0 90.0 jit_solution(8849939044450382123)
XLA Ops:
  0.7 83.3 %shard_map.339 = (f32[2,7,7,2,768]{4,3,2,1,0:T(2,128)}, f32[6,3,3,2,768]{4,3,2,1,0:T(2,128)}, f32[2,14,14,2,384]{4,3,2,1,0:T(2,128)}, f32[6,6,6,2,384]{4,3,2,1,0...) custom-call(bf16[8,14,14,2,384]{4,3,2,1,0:T(2,128)(2,1)} %bitcast.21, ...), custom_call_target="tpu_custom_call" | custom-call | tf_op jit(solution)/shard_map/pallas_call | solution.py:1027
  83.9 5.9 %shard_map.340 = (f32[2,7,7,2,768]{4,3,2,1,0:T(2,128)}, f32[6,3,3,2,768]{4,3,2,1,0:T(2,128)}, f32[2,14,14,2,384]{4,3,2,1,0:T(2,128)}, f32[6,6,6,2,384]{4,3,2,1,0...) custom-call(f32[48,128]{1,0:T(8,128)} %get-tuple-element.46.refs_0_,, ...), custom_call_target="tpu_custom_call" | custom-call | tf_op jit(solution)/shard_map/pallas_call | solution.py:1010

commit v4 on v3

--- a/solution.py
+++ b/solution.py
@@ -630,7 +630,7 @@
         return 0
 
     held(0)
-    lax.fori_loop(0, ROWS // TILE, up_tile, 0)
+    unrolled(ROWS // TILE, up_tile)
     held(1)
 
     def branch_tile(index, _):
@@ -638,7 +638,7 @@
         branch[rows, :] = nn(hidden[rows, :], flat(w_all[1])) * DOWN_SCALE + vector_row(V_BIAS_DOWN)
         return 0
 
-    lax.fori_loop(0, ROWS // TILE, branch_tile, 0)
+    unrolled(ROWS // TILE, branch_tile)
 
     def scaled(value, factor):
         return (value.reshape(-1, 8, C) * factor[None]).reshape(-1, C)
@@ -799,7 +799,7 @@
         at_step(index, [(2, events((sum_core, 1))), (3, events((sum_plane, 2)))])
         return 0
 
-    lax.fori_loop(0, ROWS // TILE, down_tile, 0)
+    unrolled(ROWS // TILE, down_tile)
 
     def up_grad(index, _):
         span = pl.ds(aligned(index * C, 128), C)

time: 90.2 us -> 89.3 us (0.990)
  no operation moved by 1% of the time
where the time goes in v4:
time: 89.3 us; the launch traced here: 89.1 us
  Pallas kernels  88.3 us (99%)
    pallas_call x1, Pallas kernels, fused_step(): pl.pallas_call(step_kernel, out_shape=(shape((2, 7, 7, 2, C2), F32), shap...  82.4 us
    pallas_call x1, Pallas kernels, finish(): pl.pallas_call(functools.partial(finish_kernel, rates), out_shape=[jax.Sh...  5.89 us

profile of v4, /device:TPU:0, one launch (start us, length us, event | category | flops | bytes accessed | tf_op | source)
XLA Modules:
  0.0 89.1 jit_solution(1694243001563728410)
XLA Ops:
  0.7 82.4 %shard_map.339 = (f32[2,7,7,2,768]{4,3,2,1,0:T(2,128)}, f32[6,3,3,2,768]{4,3,2,1,0:T(2,128)}, f32[2,14,14,2,384]{4,3,2,1,0:T(2,128)}, f32[6,6,6,2,384]{4,3,2,1,0...) custom-call(bf16[8,14,14,2,384]{4,3,2,1,0:T(2,128)(2,1)} %bitcast.21, ...), custom_call_target="tpu_custom_call" | custom-call | tf_op jit(solution)/shard_map/pallas_call | solution.py:1027
  83.1 5.9 %shard_map.340 = (f32[2,7,7,2,768]{4,3,2,1,0:T(2,128)}, f32[6,3,3,2,768]{4,3,2,1,0:T(2,128)}, f32[2,14,14,2,384]{4,3,2,1,0:T(2,128)}, f32[6,6,6,2,384]{4,3,2,1,0...) custom-call(f32[48,128]{1,0:T(8,128)} %get-tuple-element.46.refs_0_,, ...), custom_call_target="tpu_custom_call" | custom-call | tf_op jit(solution)/shard_map/pallas_call | solution.py:1010
